TPU v7x, 128 devices: a whole 4x4x4 slice. The times are simulated.
128 devices in a mesh: member: 2 (over x_lo), dp: 64 (over y, x_hi, z, core).
Axes of the slice: x: 4 (x_hi: 2, x_lo: 2; x = x_hi * 2 + x_lo), y: 4, z: 4, core: 2. Of those that a mesh axis runs over, the one named last changes fastest.
Arguments:
- features: bfloat16 [256, 256, 1024], P(('dp', 'member')), may hold values from -10 to 10
- teacher_logits: bfloat16 [4, 256, 256, 256], P('member', 'dp'), may hold values from -320 to 320
- lengths: int32 [256], P(('dp', 'member')), may hold values from 16 to 256
- gain_conv: float32 [1024], replicated, may hold values from 0.5 to 1.5
- weight_in: bfloat16 [1024, 2048], replicated, may hold values from -0.1875 to 0.1875
- weight_depth: float32 [31, 1024], replicated, may hold values from -1 to 1
- weight_out: bfloat16 [1024, 1024], replicated, may hold values from -0.1875 to 0.1875
- gain_out: float32 [1024], replicated, may hold values from 0.5 to 1.5
- head_weight: bfloat16 [1024, 256], replicated, may hold values from -1 to 1
Outputs:
- grad_gain_conv: float32 [1024], replicated
- grad_weight_in: float32 [1024, 2048], replicated
- grad_weight_depth: float32 [31, 1024], replicated
- grad_weight_out: float32 [1024, 1024], replicated
- grad_gain_out: float32 [1024], replicated
- grad_head: float32 [1024, 256], replicated
- utt_loss: float32 [256], P(('dp', 'member'))
All inputs are finite; a program needn't handle non-finite values.
Results may differ from a plain program's by a relative error of at most 0.015.
Values may be sent and summed in bfloat16 or wider, within the bound.
A program may use at most 128 MiB of HBM per device.

v0:
```python
import jax
import jax.numpy as jnp
from jax import lax
from jax.sharding import PartitionSpec as P

TEACHERS = 4


def normalize(values, gain):
    average = jnp.mean(values, axis=-1, keepdims=True)
    centred = values - average
    spread = jnp.mean(centred * centred, axis=-1, keepdims=True)
    return centred * lax.rsqrt(spread + 1e-05) * gain


def live_frames(lengths, frames):
    return (jnp.arange(frames, dtype=jnp.int32)[None, :] < lengths[:, None]).astype(jnp.float32)


def lower_part(conv_weights, features, lengths):
    gain_conv, weight_in, weight_depth, weight_out = conv_weights
    utterances, frames, model_width = features.shape
    widened = features.astype(jnp.float32)
    normed = (
        normalize(widened, gain_conv).astype(jnp.bfloat16).reshape(utterances * frames, model_width)
    )
    projected = jnp.dot(normed, weight_in, preferred_element_type=jnp.float32)
    live_mask = live_frames(lengths, frames)
    gated = (projected[:, :model_width] * jax.nn.sigmoid(projected[:, model_width:])).reshape(
        utterances, frames, model_width
    ) * live_mask[:, :, None]
    half_width = weight_depth.shape[0] // 2
    convolved = lax.conv_general_dilated(
        gated,
        weight_depth[:, None, :],
        (1,),
        [(half_width, half_width)],
        dimension_numbers=("NWC", "WIO", "NWC"),
        feature_group_count=model_width,
        precision=lax.Precision.HIGHEST,
    )
    activated = (
        (convolved * jax.nn.sigmoid(convolved))
        .astype(jnp.bfloat16)
        .reshape(utterances * frames, model_width)
    )
    update = jnp.dot(activated, weight_out, preferred_element_type=jnp.float32)
    return widened + update.reshape(utterances, frames, model_width)


def upper_part(top_weights, residual_sum, target, lengths, mean_frames):
    gain_out, head_weight = top_weights
    utterances, frames, model_width = residual_sum.shape
    final_norm = (
        normalize(residual_sum, gain_out)
        .astype(jnp.bfloat16)
        .reshape(utterances * frames, model_width)
    )
    student_logits = jnp.dot(final_norm, head_weight, preferred_element_type=jnp.float32)
    student_logp = jax.nn.log_softmax(student_logits, axis=-1).reshape(utterances, frames, -1)
    cross_entropy = -jnp.sum(target * student_logp, axis=-1)
    return jnp.sum(cross_entropy * live_frames(lengths, frames), axis=-1) / mean_frames


def student_losses(weights, features, target, lengths, mean_frames):
    residual_sum = lower_part(weights[:4], features, lengths)
    return upper_part(weights[4:], residual_sum, target, lengths, mean_frames)


def teacher_target(summed):
    return jnp.exp(jax.nn.log_softmax(summed / TEACHERS, axis=-1))


def on_device(
    features,
    teacher_logits,
    lengths,
    gain_conv,
    weight_in,
    weight_depth,
    weight_out,
    gain_out,
    head_weight,
):
    frame_total = lax.psum(jnp.sum(lengths.astype(jnp.float32)), ("member", "dp"))
    own_count = lengths.shape[0]
    mean_frames = frame_total / (own_count * lax.axis_size("member") * lax.axis_size("dp"))
    local_sum = jnp.sum(jax.nn.log_softmax(teacher_logits.astype(jnp.float32), axis=-1), axis=0)
    group_sum = lax.psum(local_sum, "member")
    own_sum = lax.dynamic_slice_in_dim(
        group_sum, lax.axis_index("member") * own_count, own_count, 0
    )
    target = teacher_target(own_sum)
    weights = (gain_conv, weight_in, weight_depth, weight_out, gain_out, head_weight)

    def local_loss(trainable):
        return student_losses(trainable, features, target, lengths, mean_frames)

    losses, pullback = jax.vjp(local_loss, weights)
    gradients = pullback(jnp.ones_like(losses))[0]
    totals = lax.psum(
        (
            gradients[0],
            gradients[1].astype(jnp.float32),
            gradients[2],
            gradients[3].astype(jnp.float32),
            gradients[4],
            gradients[5].astype(jnp.float32),
        ),
        ("member", "dp"),
    )
    return (totals[0], totals[1], totals[2], totals[3], totals[4], totals[5], losses)


def solution(mesh):
    in_specs = (
        P(("dp", "member"), None, None),
        P("member", "dp", None, None),
        P(("dp", "member")),
        P(),
        P(),
        P(),
        P(),
        P(),
        P(),
    )
    out_specs = (P(), P(), P(), P(), P(), P(), P(("dp", "member")))
    return jax.shard_map(
        on_device, mesh=mesh, in_specs=in_specs, out_specs=out_specs, check_vma=False
    )
```

profile of v0, /device:TPU:1, one launch (start us, length us, event | category | flops | bytes accessed | tf_op | source)
XLA Modules:
  0.0 415.8 jit_solution(1241103938338909669)
XLA Ops:
  7.2 1.6 reduce_max.35
  8.9 14.1 %fusion.27 = f32[4,256,256]{2,1,0:T(8,128)} fusion(bf16[2,4,256,256]{3,2,1,0:T(8,128)(2,1)} %param.10, f32[2,4,256]{2,1,0:T(4,128)S(1)} %reduce_max.36), kind=kOutput, calls=%fused_computation.43 | output fusion | flops 2885887 | bytes 2105344 | tf_op jit(solution)/shard_map/jit(log_softmax)/reduce_sum | solution.py:88
  23.0 0.6 convert_reduce_fusion.1
  23.7 69.0 %psum.57 = f32[]{:T(128)} all-reduce(f32[]{:T(128)} %convert_reduce_fusion.1), channel_id=1, replica_groups=mesh['member'=2,'dp'=64] {'member','dp'}, use_global_device_ids=true, to_apply=%region_9.10 | all-reduce | flops 1 | bytes 8 | tf_op jit(solution)/shard_map/psum | solution.py:85
  93.7 1.0 copy-done.24
  94.8 0.5 copy-done.18
  95.2 2.4 fusion.73
  97.6 0.7 slice_multiply_fusion.1
  98.3 1.3 copy-done.4
  99.8 1.4 copy-done.11
  101.2 1.6 copy.69
  102.8 0.8 pad.8.clone
  103.6 0.6 slice.17
  104.2 1.9 fusion.3
  106.1 11.0 %multiply_convert_fusion = (bf16[16,36,1024]{2,0,1:T(8,128)(2,1)S(1)}, f32[16,36,1024]{2,0,1:T(8,128)}, f32[16,36,1024]{2,0,1:T(8,128)}, f32[16,36,1024]{2,0,1:T(8,128)}) fusion(f32[31,1,1024]{2,0,1:T(8,128)S(1)} %bitcast.83, f32[2,8,66,1024]{3,0,2,1:T(2,128)S(1)} %fusion.3, pred[16,36]{0,1:T(8,128)(4,1)S(1)} %copy-done.32), kind=kOutput, calls=%fused_computation.32 | convolution fusion | flops 224133120 | bytes 12710464 | tf_op jit(solution)/shard_map/jvp()/conv_general_dilated | solution.py:33
  117.2 1.7 copy.49
  118.9 2.7 reshape.152
  121.6 2.6 fusion.71
  125.5 1.0 copy-done.7
  126.5 0.5 fusion.72
  127.0 0.8 copy-done.9
  128.1 2.9 copy.56
  130.9 2.9 reshape.165
  133.8 1.7 copy-done.20
  135.5 2.9 copy.50
  138.3 2.9 reshape.161
  141.2 1.7 copy-done.19
  142.9 2.9 copy.53
  145.7 3.0 reshape.163
  149.5 2.0 subtract_subtract_fusion
  151.5 1.3 fusion.46
  152.8 2.1 fusion.70
  155.3 1.4 fusion.45
  156.7 0.5 fusion.75
  157.2 0.5 fusion.24
  157.7 1.1 fusion.25
  158.8 0.7 broadcast_add_fusion
  159.5 1.3 fusion.74
  161.1 0.6 slice-done.2
  161.7 0.9 slice-done
  162.7 9.6 %fusion.31 = f32[2,256,1024]{2,0,1:T(2,128)S(1)} fusion(f32[2,256,1024]{2,1,0:T(8,128)S(1)} %slice-done, f32[2,256,1024]{2,1,0:T(8,128)S(1)} %slice-done.2, f32[2,256,1024]{2,1,0:T(8,128)S(1)} %slice-done.1, f32[2,256,1024]{2,1,0:T(8,128)S(1)} %convert.9), kind=kLoop, calls=%fused_computation.50 | loop fusion | flops 2097152 | bytes 10485760 | tf_op jit(solution)/shard_map/transpose(jvp())/add_any | solution.py:43
  172.2 27.8 %fusion.68 = f32[31,1,1024]{2,1,0:T(1,128)S(1)} fusion(f32[2,256,1024]{2,0,1:T(2,128)S(1)} %fusion.31, f32[2,256,1024]{2,1,0:T(8,128)S(1)} %copy-done.12), kind=kOutput, calls=%fused_computation.115 | convolution fusion | flops 189136896 | bytes 4321280 | tf_op jit(solution)/shard_map/transpose(jvp())/conv_general_dilated | solution.py:33
  200.0 0.8 pad.10
  200.8 0.5 copy-done.16
  201.3 3.3 fusion.35
  204.6 0.7 copy.98
  205.3 1.4 copy.59
  206.9 5.5 %fusion.39 = f32[16,36,1024]{2,0,1:T(8,128)S(1)} fusion(f32[2,7,30,1024]{3,1,0,2:T(8,128)S(1)} %slice.22, f32[2,8,36,1024]{3,1,0,2:T(8,128)S(1)} %copy.59, pred[16,36]{0,1:T(8,128)(4,1)S(1)} %copy-done.32, f32[31,1024,1]{1,0,2:T(8,128)S(1)} %bitcast.84), kind=kOutput, calls=%fused_computation.67 | convolution fusion | flops 223248384 | bytes 6566464 | tf_op jit(solution)/shard_map/transpose(jvp())/conv_general_dilated | solution.py:33
  212.3 2.9 copy.61
  215.2 3.1 reshape.159
  218.3 1.9 slice_multiply_fusion
  220.3 0.9 copy-done.5
  221.1 1.0 fusion.26
  222.3 5.8 %convert_convert_fusion = f32[1024,2048]{1,0:T(8,128)} fusion(bf16[512,1024]{1,0:T(8,128)(2,1)S(1)} %bitcast.80, f32[512,1024]{1,0:T(8,128)S(1)} %get-tuple-element.18, f32[512,1024]{1,0:T(8,128)S(1)} %get-tuple-element.17), kind=kOutput, calls=%fused_computation.15 | convolution fusion | flops 2152726528 | bytes 13631488 | tf_op jit(solution)/shard_map/transpose(jvp())/dot_general | solution.py:27
  228.2 1.6 copy-done.14
  229.7 5.2 %fusion.22 = f32[1024]{0:T(1024)S(1)} fusion(bf16[2,256,1024]{2,1,0:T(8,128)(2,1)S(1)} %copy-done.6, f32[2,256]{1,0:T(2,128)S(1)} %add_rsqrt_fusion, f32[2,256]{1,0:T(2,128)S(1)} %broadcast_multiply_fusion.3, bf16[1024,2048]{1,0:T(8,128)(2,1)} %param.13, f32[512,1024]{1,0:T(8,128)} %copy-done.15, f32[512,1024]{1,0:T(8,128)S(1)} %copy-done.14), kind=kOutput, calls=%fused_computation.37 | convolution fusion | flops 2152201216 | bytes 9445376 | tf_op jit(solution)/shard_map/transpose(jvp())/dot_general | solution.py:27
  234.9 63.3 %all-reduce.2 = (f32[1024]{0:T(1024)}, f32[1024]{0:T(1024)}) all-reduce(f32[1024]{0:T(1024)S(1)} %fusion.22, f32[1024]{0:T(1024)S(1)} %get-tuple-element.7), channel_id=1, replica_groups=mesh['member'=2,'dp'=64] {'member','dp'}, use_global_device_ids=true, to_apply=%region_18.19 | all-reduce | flops 2048 | bytes 16384 | tf_op jit(solution)/shard_map/psum | solution.py:101
  298.5 0.5 broadcast_divide_fusion
  299.0 97.3 %all-reduce.9.cloned.1.call-done = (f32[1024,2048]{1,0:T(8,128)}, f32[31,1024]{1,0:T(8,128)}, f32[1024,1024]{1,0:T(8,128)}, f32[1024,256]{1,0:T(8,128)}) async-done(((f32[1024,2048]{1,0:T(8,128)}, f32[31,1024]{1,0:T(8,128)}, f32[1024,1024]{1,0:T(8,128)}, f32[1024,256]{1,0:T(8,128)}), (f32[1024,2048]{1,0:T(8,128)}, f32[31,1024]{1,0:T(8,128)}, f32[1024,1024]{1,0:T(8,128)}, ...) | async-done | bytes 13758480 | tf_op jit(solution)/shard_map/psum | solution.py:101
  396.3 8.0 %copy.104 = f32[1024,2048]{1,0:T(8,128)} copy(f32[1024,2048]{1,0:T(8,128)} %get-tuple-element.29) | data formatting | bytes 16777216
  404.3 0.7 copy.105
  405.0 2.1 copy.106
  407.1 1.0 copy.107
  408.1 0.7 copy-done.1
  (87 shorter events, 4.2 us)
Async XLA Ops:
  7.2 114.4 %copy-start = (bf16[1024,1024]{1,0:T(8,128)(2,1)S(1)}, bf16[1024,1024]{1,0:T(8,128)(2,1)}, u32[]{:S(2)}) copy-start(bf16[1024,1024]{1,0:T(8,128)(2,1)} %param.15) | copy-start | bytes 6291460
  7.2 144.3 %all-reduce.7.cloned.1.call-start = ((), (), s32[]{:S(2)}) async-start(), calls=%async_computation | async-start | bytes 2097152 | tf_op jit(solution)/shard_map/psum | solution.py:89
  8.8 14.2 %copy-start.29 = (s32[2]{0:T(128)S(1)}, s32[2]{0:T(128)}, u32[]{:S(2)}) copy-start(s32[2]{0:T(128)} %param.11) | copy-start | bytes 28
  8.9 83.8 %copy-start.6 = (bf16[2,256,1024]{2,1,0:T(8,128)(2,1)S(1)}, bf16[2,256,1024]{2,1,0:T(8,128)(2,1)}, u32[]{:S(2)}) copy-start(bf16[2,256,1024]{2,1,0:T(8,128)(2,1)} %param.9) | copy-start | bytes 3145732
  22.9 70.4 %copy-start.30 = (f32[1024]{0:T(1024)S(1)}, f32[1024]{0:T(1024)}, u32[]{:S(2)}) copy-start(f32[1024]{0:T(1024)} %param.12) | copy-start | bytes 12292
  23.0 373.3 %all-reduce.9.cloned.1.call-start = ((), (), s32[]{:S(2)}) async-start(), calls=%async_computation.1 | async-start | bytes 27525120 | tf_op jit(solution)/shard_map/psum | solution.py:101
  92.7 2.6 copy-start.18
  93.7 1.1 copy-start.24
  97.6 2.0 copy-start.4
  99.8 1.4 copy-start.11
  104.2 1.9 copy-start.31
  104.2 1.9 copy-start.32
  124.2 1.3 copy-start.2
  124.2 0.7 copy-start.28
  124.6 1.9 copy-start.22
  125.5 1.0 copy-start.7
  125.5 2.5 copy-start.21
  127.0 0.8 copy-start.9
  133.8 1.7 copy-start.20
  141.2 1.7 copy-start.19
  151.5 3.5 copy-start.10
  151.5 3.7 copy-start.8
  155.0 1.7 copy-start.23
  155.3 2.0 copy-start.3
  159.5 1.6 slice-start.1
  159.5 2.2 slice-start.2
  160.8 1.8 slice-start
  162.7 9.6 %copy-start.12 = (f32[2,256,1024]{2,1,0:T(8,128)S(1)}, f32[2,256,1024]{2,1,0:T(8,128)}, u32[]{:S(2)}) copy-start(f32[2,256,1024]{2,1,0:T(8,128)} %copy-done.11) | copy-start | bytes 6291460
  200.0 1.3 copy-start.16
  218.3 2.8 copy-start.5
  221.1 1.2 copy-start.25
  222.1 6.0 %copy-start.13 = (f32[512,1024]{1,0:T(8,128)}, f32[512,1024]{1,0:T(8,128)S(1)}, u32[]{:S(2)}) copy-start(f32[512,1024]{1,0:T(8,128)S(1)} %get-tuple-element.17) | copy-start | bytes 6291460
  222.1 6.0 %copy-start.15 = (f32[512,1024]{1,0:T(8,128)}, f32[512,1024]{1,0:T(8,128)S(1)}, u32[]{:S(2)}) copy-start(f32[512,1024]{1,0:T(8,128)S(1)} %get-tuple-element.18) | copy-start | bytes 6291460
  228.1 1.6 copy-start.14
  396.3 8.0 %copy-start.27 = (f32[31,1024]{1,0:T(8,128)S(1)}, f32[31,1024]{1,0:T(8,128)}, u32[]{:S(2)}) copy-start(f32[31,1024]{1,0:T(8,128)} %get-tuple-element.30) | copy-start | bytes 380932
  396.3 8.7 %copy-start.17 = (f32[1024,1024]{1,0:T(8,128)S(1)}, f32[1024,1024]{1,0:T(8,128)}, u32[]{:S(2)}) copy-start(f32[1024,1024]{1,0:T(8,128)} %get-tuple-element.31) | copy-start | bytes 12582916
  405.0 2.1 copy-start.26
  405.0 3.8 copy-start.1
Sparse Core Ops, SparseCore 0:
  23.1 50.1 all-reduce.6
  228.3 167.9 all-reduce.8
where the time goes:
time: 419 us; the launch traced here: 416 us
  blocking collectives  132 us (32%)
  waiting for transfers between devices  97.3 us (23%)
  matrix products  67.2 us (16%)
  local copies, waits for them, and re-layouts  60.9 us (15%)
  other arithmetic  42.6 us (10%)
  between operations  15.5 us (4%)
    psum x1, waiting for transfers between devices, on_device(): lax.psum((gradients[0], gradients[1].astype(jnp.float32), gradients[2], g...  97.3 us
    psum x1, blocking collectives, on_device(): lax.psum(jnp.sum(lengths.astype(jnp.float32)), ('member', 'dp'))  69 us
    psum x1, blocking collectives, on_device(): lax.psum((gradients[0], gradients[1].astype(jnp.float32), gradients[2], g...  63.3 us
    conv_general_dilated x3, matrix products, lower_part(): lax.conv_general_dilated(gated, weight_depth[:, None, :], (1,), [(half_wi...  44.3 us
    unnamed x73, local copies, waits for them, and re-layouts  27.9 us
    conv_general_dilated x9, local copies, waits for them, and re-layouts, lower_part(): lax.conv_general_dilated(gated, weight_depth[:, None, :], (1,), [(half_wi...  14.6 us
    reduce_sum x1, other arithmetic, on_device(): jax.nn.log_softmax(teacher_logits.astype(jnp.float32), axis=-1)  14.1 us
    dot_general x3, matrix products, lower_part(): projected = jnp.dot(normed, weight_in, preferred_element_type=jnp.float32)  13.4 us
  transfers between devices with their start and end apart: 2, of which 1 were waited for; matrix products, arithmetic and copies ran while one was open for 13% of the time, Pallas kernels for 0%

commit v1 on v0

v1 whole, which is shorter than its diff:
```python
import functools
import math

import jax
import jax.numpy as jnp
import numpy as np
from jax import lax
from jax.experimental import pallas as pl
from jax.experimental.pallas import tpu as pltpu
from jax.sharding import PartitionSpec as P

D, V, TAPS, FRAMES, UTT = 1024, 256, 31, 256, 2
TOK = UTT * FRAMES
PERIOD, HALF, ROWS = 272, 144, 288
TILE = 256
SLABS = 28
F32, BF16 = jnp.float32, jnp.bfloat16
VM = pl.BlockSpec(memory_space=pltpu.VMEM)
SM = pl.BlockSpec(memory_space=pltpu.SMEM)


def transforms():
    freq = np.arange(PERIOD // 2 + 1)
    time = np.arange(FRAMES)
    angle = 2 * np.pi * np.outer(freq, time) / PERIOD
    analysis = np.zeros((ROWS, FRAMES))
    analysis[: freq.size] = np.cos(angle)
    analysis[HALF : HALF + freq.size] = np.sin(angle)
    lag = np.arange(TAPS) - TAPS // 2
    weight = np.where((freq == 0) | (freq == PERIOD // 2), 1.0, 2.0)[:, None] / PERIOD
    turn = 2 * np.pi * np.outer(freq, lag) / PERIOD
    taps = np.zeros((ROWS, TAPS + 1))
    taps[: freq.size, :TAPS] = np.cos(turn) * weight
    taps[HALF : HALF + freq.size, :TAPS] = np.sin(turn) * weight
    lags = np.zeros((ROWS, 128))
    lags[:, : TAPS + 1] = taps
    bf = lambda v: jnp.asarray(v, F32).astype(BF16)
    return bf(analysis), bf(analysis.T), jnp.asarray(taps, F32), bf(lags)


def dot(a, b):
    return jnp.dot(a, b, preferred_element_type=F32)


def dot_bt(a, b):
    return lax.dot_general(a, b, (((1,), (1,)), ((), ())), preferred_element_type=F32)


def dot_at(a, b):
    return lax.dot_general(a, b, (((0,), (0,)), ((), ())), preferred_element_type=F32)


def sigmoid(v):
    return 1.0 / (1.0 + jnp.exp(-v))


def rows_loop(total, step, body):
    def run(i, c):
        body(pl.ds(pl.multiple_of(i * step, step), step), i)
        return c

    lax.fori_loop(0, total // step, run, 0)


def forward_kernel(
    len_ref, x_ref, g1_ref, win_ref, taps_ref, wout_ref, g2_ref, head_ref, tm_ref, c_ref, ct_ref,
    normed_ref, a_ref, s_ref, spec_ref, fac_ref, act_ref, z_ref, rstd_ref, fn_ref, logit_ref,
    taps32, res,
):
    taps32[...] = jnp.zeros_like(taps32)
    taps32[0:TAPS, :] = taps_ref[...]

    def norm_rows(rows, i):
        v = x_ref[rows, :].astype(F32)
        v = v - jnp.mean(v, axis=-1, keepdims=True)
        v = v * lax.rsqrt(jnp.mean(v * v, axis=-1, keepdims=True) + 1e-5)
        normed_ref[rows, :] = (v * g1_ref[...]).astype(BF16)

    rows_loop(TOK, 32, norm_rows)

    def channel_tile(cb, carry):
        cols = pl.ds(pl.multiple_of(cb * TILE, TILE), TILE)
        gate_cols = pl.ds(pl.multiple_of(D + cb * TILE, TILE), TILE)
        hat = jnp.dot(
            tm_ref[...], taps32[:, cols], preferred_element_type=F32, precision=lax.Precision.HIGHEST
        )
        hr, hi = hat[:HALF], hat[HALF:]
        for u in range(UTT):
            rows = pl.ds(u * FRAMES, FRAMES)
            live = lax.broadcasted_iota(jnp.int32, (FRAMES, TILE), 0) < len_ref[u]
            nu = normed_ref[rows, :]
            a = dot(nu, win_ref[:, cols])
            s = sigmoid(dot(nu, win_ref[:, gate_cols]))
            a = jnp.where(live, a, 0.0)
            s_ref[rows, cols] = s.astype(BF16)
            a_ref[rows, cols] = a.astype(BF16)
            sp = dot(c_ref[...], (a * s).astype(BF16))
            spec_ref[u, :, cols] = sp.astype(BF16)
            xr, xi = sp[:HALF], sp[HALF:]
            prod = jnp.concatenate([xr * hr + xi * hi, xi * hr - xr * hi], axis=0)
            conv = dot(ct_ref[...], prod.astype(BF16))
            sg = sigmoid(conv)
            act_ref[rows, cols] = (conv * sg).astype(BF16)
            fac_ref[rows, cols] = (sg * (1.0 + conv * (1.0 - sg))).astype(BF16)
        return carry

    lax.fori_loop(0, D // TILE, channel_tile, 0)

    def out_tile(cb, carry):
        cols = pl.ds(pl.multiple_of(cb * TILE, TILE), TILE)
        res[:, cols] = x_ref[:, cols].astype(F32) + dot(act_ref[...], wout_ref[:, cols])
        return carry

    lax.fori_loop(0, D // TILE, out_tile, 0)

    def norm_out(rows, i):
        v = res[rows, :]
        v = v - jnp.mean(v, axis=-1, keepdims=True)
        r = lax.rsqrt(jnp.mean(v * v, axis=-1, keepdims=True) + 1e-5)
        z = v * r
        z_ref[rows, :] = z.astype(BF16)
        rstd_ref[rows, :] = jnp.broadcast_to(r, (32, 128))
        fn_ref[rows, :] = (z * g2_ref[...]).astype(BF16)

    rows_loop(TOK, 32, norm_out)
    logit_ref[...] = dot(fn_ref[...], head_ref[...])


def softmax_parts(v):
    m = jnp.max(v, axis=-1, keepdims=True)
    e = jnp.exp(v - m)
    return m, e, jnp.sum(e, axis=-1, keepdims=True)


def backward_kernel(
    len_ref, own_ref, got_ref, logit_ref, fn_ref, z_ref, rstd_ref, act_ref, fac_ref, spec_ref, s_ref, a_ref,
    normed_ref, win_ref, taps_ref, wout_ref, g2_ref, head_ref, tm_ref, c_ref, ct_ref, lag_ref,
    grad_ref, loss_ref,
    taps32, dl, dz, dr, dp, gain1, left,
):
    taps32[...] = jnp.zeros_like(taps32)
    taps32[0:TAPS, :] = taps_ref[...]
    gain1[...] = jnp.zeros_like(gain1)

    for u in range(UTT):
        length = len_ref[u]

        def loss_rows(i, total):
            rows = pl.ds(pl.multiple_of(i * 32, 32), 32)
            flat = pl.ds(pl.multiple_of(u * FRAMES + i * 32, 32), 32)
            summed = jnp.zeros((32, V), F32)
            for ref in (own_ref, got_ref):
                for k in range(2):
                    t = ref[k, u, rows, :].astype(F32)
                    m, _, z = softmax_parts(t)
                    summed = summed + (t - m - jnp.log(z))
            _, e, z = softmax_parts(summed * 0.25)
            target = e / z
            lg = logit_ref[flat, :]
            m, e, z = softmax_parts(lg)
            live = i * 32 + lax.broadcasted_iota(jnp.int32, (32, V), 0) < length
            ce = jnp.sum(jnp.where(live, target * (m + jnp.log(z) - lg), 0.0), axis=0, keepdims=True)
            mass = jnp.sum(target, axis=-1, keepdims=True)
            dl[flat, :] = jnp.where(live, e * (mass / z) - target, 0.0).astype(BF16)
            return total + ce

        total = lax.fori_loop(0, FRAMES // 32, loss_rows, jnp.zeros((1, V), F32))
        loss_ref[u : u + 1, :] = jnp.broadcast_to(jnp.sum(total, axis=-1, keepdims=True), (1, 128))

    def head_tile(cb, carry):
        cols = pl.ds(pl.multiple_of(cb * TILE, TILE), TILE)
        rows = cols
        dz[:, cols] = dot_bt(dl[...], head_ref[rows, :])
        dh = dot_at(fn_ref[:, cols], dl[...])
        grad_ref[24, rows, :] = dh[:, :128].astype(BF16)
        grad_ref[25, rows, :] = dh[:, 128:].astype(BF16)
        left[1, rows, :] = jnp.broadcast_to(
            jnp.sum(dh * head_ref[rows, :].astype(F32), axis=-1, keepdims=True), (TILE, 128)
        )
        return carry

    lax.fori_loop(0, D // TILE, head_tile, 0)

    def norm_rows(rows, i):
        g = dz[rows, :] * g2_ref[...]
        z = z_ref[rows, :].astype(F32)
        r = rstd_ref[rows, :][:, :1]
        m1 = jnp.mean(g, axis=-1, keepdims=True)
        m2 = jnp.mean(g * z, axis=-1, keepdims=True)
        dr[rows, :] = (r * (g - m1 - z * m2)).astype(BF16)

    rows_loop(TOK, 32, norm_rows)

    def conv_tile(cb, carry):
        cols = pl.ds(pl.multiple_of(cb * TILE, TILE), TILE)
        gate_cols = pl.ds(pl.multiple_of(D + cb * TILE, TILE), TILE)
        hat = jnp.dot(
            tm_ref[...], taps32[:, cols], preferred_element_type=F32, precision=lax.Precision.HIGHEST
        )
        hr, hi = hat[:HALF], hat[HALF:]
        q = jnp.zeros((ROWS, TILE), F32)
        for u in range(UTT):
            rows = pl.ds(u * FRAMES, FRAMES)
            dact = dot_bt(dr[rows, :], wout_ref[cols, :])
            dc = (dact * fac_ref[rows, cols].astype(F32)).astype(BF16)
            sp = dot(c_ref[...], dc)
            er, ei = sp[:HALF], sp[HALF:]
            x = spec_ref[u, :, cols].astype(F32)
            xr, xi = x[:HALF], x[HALF:]
            q = q + jnp.concatenate([er * xr + ei * xi, er * xi - ei * xr], axis=0)
            back = jnp.concatenate([er * hr - ei * hi, ei * hr + er * hi], axis=0)
            dg = dot(ct_ref[...], back.astype(BF16))
            live = lax.broadcasted_iota(jnp.int32, (FRAMES, TILE), 0) < len_ref[u]
            s = s_ref[rows, cols].astype(F32)
            a = a_ref[rows, cols].astype(F32)
            ds = jnp.where(live, dg * s, 0.0)
            dp[rows, cols] = ds.astype(BF16)
            dp[rows, gate_cols] = (ds * a * (1.0 - s)).astype(BF16)
        left[0, cols, :] = dot_at(q.astype(BF16), lag_ref[...])
        dw = dot_at(act_ref[:, cols], dr[...])
        for j in range(8):
            grad_ref[16 + j, cols, :] = dw[:, j * 128 : (j + 1) * 128].astype(BF16)
        return carry

    lax.fori_loop(0, D // TILE, conv_tile, 0)

    def in_tile(n, carry):
        cols = pl.ds(pl.multiple_of(n * TILE, TILE), TILE)
        dw = dot_at(normed_ref[...], dp[:, cols])
        grad_ref[2 * n] = dw[:, :128].astype(BF16)
        grad_ref[2 * n + 1] = dw[:, 128:].astype(BF16)
        w = dw * win_ref[:, cols].astype(F32)
        gain1[...] += w[:, :128] + w[:, 128:]
        return carry

    lax.fori_loop(0, 2 * D // TILE, in_tile, 0)

    count = len_ref[0] + len_ref[1]

    def small_rows(rows, i):
        lane = lax.broadcasted_iota(jnp.int32, (128, 128), 1)
        bit = jnp.right_shift(count, jnp.clip(lane - 64, 0, 15)) & 1
        g1 = jnp.sum(gain1[rows, :], axis=-1, keepdims=True)
        out = jnp.where(lane < TAPS, left[0, rows, :], 0.0)
        out = jnp.where(lane == 32, g1, out)
        out = jnp.where(lane == 33, left[1, rows, :], out)
        out = jnp.where((lane >= 64) & (lane < 74), bit.astype(F32), out)
        grad_ref[26, rows, :] = out.astype(BF16)
        grad_ref[27, rows, :] = jnp.zeros((128, 128), BF16)

    rows_loop(D, 128, small_rows)


def compute(features, own, got, lengths, gain_conv, weight_in, weight_depth, weight_out, gain_out, head):
    analysis, synthesis, tapm, lagm = transforms()
    sd = jax.ShapeDtypeStruct
    cp = pltpu.CompilerParams(vmem_limit_bytes=60 << 20)
    g1, g2 = gain_conv.reshape(1, D), gain_out.reshape(1, D)
    fwd = pl.pallas_call(
        forward_kernel,
        name="forward",
        out_shape=(
            sd((TOK, D), BF16), sd((TOK, D), BF16), sd((TOK, D), BF16), sd((UTT, ROWS, D), BF16),
            sd((TOK, D), BF16), sd((TOK, D), BF16), sd((TOK, D), BF16), sd((TOK, 128), F32),
            sd((TOK, D), BF16), sd((TOK, V), F32),
        ),
        in_specs=[SM] + [VM] * 10,
        out_specs=[VM] * 10,
        scratch_shapes=[pltpu.VMEM((32, D), F32), pltpu.VMEM((TOK, D), F32)],
        compiler_params=cp,
        cost_estimate=pl.CostEstimate(flops=4 * 10**9, bytes_accessed=20 << 20, transcendentals=2 << 20),
    )
    normed, a, s, spec, fac, act, z, rstd, fn, logit = fwd(
        lengths, features.reshape(TOK, D), g1, weight_in, weight_depth, weight_out, g2, head,
        tapm, analysis, synthesis,
    )
    bwd = pl.pallas_call(
        backward_kernel,
        name="backward",
        out_shape=(sd((SLABS, D, 128), BF16), sd((UTT, 128), F32)),
        in_specs=[SM] + [VM] * 21,
        out_specs=[VM] * 2,
        scratch_shapes=[
            pltpu.VMEM((32, D), F32), pltpu.VMEM((TOK, V), BF16), pltpu.VMEM((TOK, D), F32),
            pltpu.VMEM((TOK, D), BF16), pltpu.VMEM((TOK, 2 * D), BF16), pltpu.VMEM((D, 128), F32),
            pltpu.VMEM((2, D, 128), F32),
        ],
        compiler_params=cp,
    )
    return bwd(
        lengths, own, got, logit, fn, z, rstd, act, fac, spec, s, a, normed, weight_in, weight_depth,
        weight_out, g2, head, tapm, analysis, synthesis, lagm,
    )


MESH = pl.DeviceIdType.MESH
COUNTS = (3, 3, 2, 2, 2, 2)
OFFSETS = (0, 3, 6, 8, 10, 12)
OWN = 14
ROUNDS = 6


def position():
    member, dp = lax.axis_index("member"), lax.axis_index("dp")
    core, z, rest = dp % 2, (dp // 2) % 4, dp // 8
    return ((rest % 2) * 2 + member, rest // 2, z), core


def device(coords, core):
    x, y, z = coords
    return {"member": x % 2, "dp": ((y * 2 + x // 2) * 4 + z) * 2 + core}


def other(c, wide):
    return 3 - c if wide else c + 1 - 2 * (c % 2)


def kept(c, kind, second):
    if kind == 0 and not second:
        return (c + c // 2) % 2
    return c % 2 if (kind == 1 and second) else c // 2


def route(coords, core, s, k):
    dim = (s // 2 + core + k // 2) % 3
    hit = [jnp.where(dim == d, 1, 0) for d in range(3)]
    c = sum(h * v for h, v in zip(hit, coords))
    kind, second = s % 2, k % 2
    p = other(c, (kind + second) % 2 == 1)
    peer = [v + h * (p - v) for h, v in zip(hit, coords)]
    return device(peer, core), kept(c, kind, second == 1)


def reduce_kernel(
    grad_ref, out_ref, pair_buf, work, *rest
):
    bufs = rest[:ROUNDS]
    pair_s, pair_r, rs_s, rs_r, ag_s, ag_r, fin_s, fin_r = rest[ROUNDS:]
    coords, core = position()
    partner = device(coords, 1 - core)
    mine = core * OWN
    theirs = (1 - core) * OWN

    barrier = pltpu.get_barrier_semaphore()
    greet = [partner]
    for d in range(3):
        for wide in (False, True):
            greet.append(device([other(v, wide) if i == d else v for i, v in enumerate(coords)], core))
    for dev in greet:
        pl.semaphore_signal(barrier, inc=1, device_id=dev, device_id_type=MESH)
    pl.semaphore_wait(barrier, len(greet))

    def copy(src, dst, send, recv, dev):
        return pltpu.make_async_remote_copy(
            src_ref=src, dst_ref=dst, send_sem=send, recv_sem=recv, device_id=dev, device_id_type=MESH
        )

    pending = []
    pairs = []
    for s in range(6):
        off, n = OFFSETS[s], COUNTS[s]
        c = copy(
            grad_ref.at[pl.ds(theirs + off, n)], pair_buf.at[pl.ds(off, n)], pair_s.at[s], pair_r.at[s], partner
        )
        c.start()
        pairs.append(c)

    starts = [jnp.int32(0)] * 6
    history = [[] for _ in range(6)]
    flying = [None] * 6

    def launch(s, k):
        half = 512 >> k
        dev, keep = route(coords, core, s, k)
        slots = pl.ds(OFFSETS[s], COUNTS[s])
        give = pl.multiple_of(starts[s] + (1 - keep) * half, 16)
        c = copy(
            work.at[slots, pl.ds(give, half)],
            bufs[k].at[pl.ds(OFFSETS[s], COUNTS[s])],
            rs_s.at[s, k], rs_r.at[s, k], dev,
        )
        c.start()
        flying[s] = c
        pending.append(c)
        starts[s] = starts[s] + keep * half
        history[s].append(dev)

    def add(dst_ref, dst_slot, dst_row, a_ref, a_slot, a_row, b_ref, b_slot, n, size):
        step = min(size, 128)

        def run(i, carry):
            r = i * step
            for j in range(n):
                d = pl.ds(pl.multiple_of(dst_row + r, 16), step)
                a = a_ref[a_slot + j, pl.ds(pl.multiple_of(a_row + r, 16), step), :]
                b = b_ref[b_slot + j, pl.ds(pl.multiple_of(r, 16), step), :]
                dst_ref[dst_slot + j, d, :] = a + b
            return carry

        lax.fori_loop(0, size // step, run, 0)

    for s in range(6):
        off, n = OFFSETS[s], COUNTS[s]
        pairs[s].wait_recv()
        add(work, off, 0, grad_ref, mine + off, 0, pair_buf, off, n, D)
        launch(s, 0)

    for k in range(ROUNDS):
        half = 512 >> k
        for s in range(6):
            off, n = OFFSETS[s], COUNTS[s]
            flying[s].wait_recv()
            if k + 1 < ROUNDS:
                add(work, off, starts[s], work, off, starts[s], bufs[k], off, n, half)
                launch(s, k + 1)
            else:
                add(out_ref, mine + off, starts[s], work, off, starts[s], bufs[k], off, n, half)
                gather(s, k, copy, out_ref, mine, starts, history, ag_s, ag_r, flying, pending)

    for k in range(ROUNDS - 1, -1, -1):
        half = 512 >> k
        for s in range(6):
            flying[s].wait_recv()
            _, keep = route(coords, core, s, k)
            starts[s] = starts[s] - keep * half
            if k > 0:
                gather(s, k - 1, copy, out_ref, mine, starts, history, ag_s, ag_r, flying, pending)
            else:
                slots = pl.ds(mine + OFFSETS[s], COUNTS[s])
                c = copy(out_ref.at[slots], out_ref.at[slots], fin_s.at[s], fin_r.at[s], partner)
                c.start()
                pending.append(c)
                flying[s] = c
    for s in range(6):
        flying[s].wait_recv()
        pairs[s].wait_send()
    for c in pending:
        c.wait_send()


def gather(s, k, copy, out_ref, mine, starts, history, ag_s, ag_r, flying, pending):
    half = 512 >> k
    slots = pl.ds(mine + OFFSETS[s], COUNTS[s])
    span = pl.ds(pl.multiple_of(starts[s], 16), half)
    c = copy(
        out_ref.at[slots, span], out_ref.at[slots, span], ag_s.at[s, k], ag_r.at[s, k], history[s][k]
    )
    c.start()
    flying[s] = c
    pending.append(c)


def reduce_all(grads):
    dma = pltpu.SemaphoreType.DMA
    return pl.pallas_call(
        reduce_kernel,
        name="reduce_all",
        out_shape=jax.ShapeDtypeStruct((SLABS, D, 128), BF16),
        in_specs=[VM],
        out_specs=VM,
        scratch_shapes=[pltpu.VMEM((OWN, D, 128), BF16)] * 2
        + [pltpu.VMEM((OWN, 512 >> k, 128), BF16) for k in range(ROUNDS)]
        + [dma((6,)), dma((6,))] + [dma((6, ROUNDS))] * 4 + [dma((6,)), dma((6,))],
        compiler_params=pltpu.CompilerParams(
            collective_id=0, has_side_effects=True, vmem_limit_bytes=48 << 20
        ),
    )(grads)


def finish_kernel(
    in_ref, mid_ref, head_ref, small_ref, loss_ref, g1_ref, g2_ref,
    win_ref, wout_ref, hw_ref, depth_ref, gain1_ref, gain2_ref, utt_ref, scale,
):
    @pl.when(pl.program_id(0) == 0)
    def _():
        first = small_ref[0, 0:16, :].astype(F32)[0:1, :]
        lane = lax.broadcasted_iota(jnp.int32, (1, 128), 1)
        place = jnp.left_shift(1, jnp.clip(lane - 64, 0, 12)).astype(F32)
        used = (lane >= 64) & (lane < 74)
        count = jnp.sum(jnp.where(used, first * place, 0.0), axis=-1, keepdims=True)
        inv = UTTS / count
        scale[...] = jnp.broadcast_to(inv, (8, 128))
        utt_ref[...] = loss_ref[...] * inv
        small = small_ref[0].astype(F32).T * inv
        depth_ref[...] = small[0:TAPS, :]
        gain1_ref[...] = small[32:33, :] / g1_ref[...]
        gain2_ref[...] = small[33:34, :] / g2_ref[...]

    inv = scale[0:1, :]
    for j in range(2):
        win_ref[:, j * 128 : (j + 1) * 128] = in_ref[j].astype(F32) * inv
        hw_ref[:, j * 128 : (j + 1) * 128] = head_ref[j].astype(F32) * inv
    wout_ref[...] = mid_ref[0].astype(F32) * inv


UTTS = 256.0


def finish(total, loss, gain_conv, gain_out):
    sd = jax.ShapeDtypeStruct
    whole = lambda *shape: pl.BlockSpec(shape, lambda i: (0,) * len(shape))
    outs = pl.pallas_call(
        finish_kernel,
        name="finish",
        grid=(8,),
        out_shape=(
            sd((D, 2 * D), F32), sd((D, D), F32), sd((D, V), F32), sd((TAPS, D), F32),
            sd((1, D), F32), sd((1, D), F32), sd((UTT, 128), F32),
        ),
        in_specs=[
            pl.BlockSpec((2, D, 128), lambda i: (i, 0, 0)),
            pl.BlockSpec((1, D, 128), lambda i: (16 + i, 0, 0)),
            pl.BlockSpec((2, 128, 128), lambda i: (12, i, 0)),
            pl.BlockSpec((1, D, 128), lambda i: (26, 0, 0)),
            whole(UTT, 128), whole(1, D), whole(1, D),
        ],
        out_specs=[
            pl.BlockSpec((D, 256), lambda i: (0, i)),
            pl.BlockSpec((D, 128), lambda i: (0, i)),
            pl.BlockSpec((128, V), lambda i: (i, 0)),
            whole(TAPS, D), whole(1, D), whole(1, D), whole(UTT, 128),
        ],
        scratch_shapes=[pltpu.VMEM((8, 128), F32)],
    )(total, total, total, total, loss, gain_conv.reshape(1, D), gain_out.reshape(1, D))
    win, wout, hw, depth, gain1, gain2, utt = outs
    return gain1.reshape(D), win, depth, wout, gain2.reshape(D), hw, utt[:, 0]


def on_device(
    features, teacher_logits, lengths, gain_conv, weight_in, weight_depth, weight_out, gain_out, head_weight
):
    member = lax.axis_index("member")
    give = lax.dynamic_slice_in_dim(teacher_logits, (1 - member) * UTT, UTT, 1)
    own = lax.dynamic_slice_in_dim(teacher_logits, member * UTT, UTT, 1)
    got = lax.ppermute(give, "member", ((0, 1), (1, 0)))
    grads, loss = compute(
        features, own, got, lengths, gain_conv, weight_in, weight_depth, weight_out, gain_out, head_weight
    )
    return finish(reduce_all(grads), loss, gain_conv, gain_out)


def solution(mesh):
    in_specs = (
        P(("dp", "member"), None, None), P("member", "dp", None, None), P(("dp", "member")),
        P(), P(), P(), P(), P(), P(),
    )
    out_specs = (P(), P(), P(), P(), P(), P(), P(("dp", "member")))
    return jax.shard_map(on_device, mesh=mesh, in_specs=in_specs, out_specs=out_specs, check_vma=False)
```

time: 419 us -> 148 us (0.35)
  Pallas kernels: 0 us -> 141 us
  blocking collectives: 132 us -> 0 us
  waiting for transfers between devices: 97.3 us -> 0.01 us
  matrix products: 67.2 us -> 0 us
  local copies, waits for them, and re-layouts: 60.9 us -> 4.18 us
  other arithmetic: 42.6 us -> 0 us
  between operations: 15.5 us -> 0.66 us
    pallas_call x0 -> x4, Pallas kernels: none -> 141 us  [the longest x1 77.2 us: reduce_all(): pl.pallas_call(reduce_kernel, name='reduce_all', out_shape=jax.ShapeDtype...]
    psum x2 -> x0, blocking collectives: 132 us -> none  [the longest x1 69 us: on_device(): lax.psum(jnp.sum(lengths.astype(jnp.float32)), ('member', 'dp'))]
    psum x2 -> x0, waiting for transfers between devices: 97.3 us -> none  [the longest x1 97.3 us: on_device(): lax.psum((gradients[0], gradients[1].astype(jnp.float32), gradients[2], g...]
    conv_general_dilated x3 -> x0, matrix products: 44.3 us -> none  [lower_part(): lax.conv_general_dilated(gated, weight_depth[:, None, :], (1,), [(half_wi...]
    unnamed x73 -> x2, local copies, waits for them, and re-layouts: 27.9 us -> 0.8 us
    dot_general x9 -> x0, matrix products: 22.9 us -> none  [the longest x3 13.4 us: lower_part(): projected = jnp.dot(normed, weight_in, preferred_element_type=jnp.float32)]
    reduce_sum x10 -> x0, other arithmetic: 19.8 us -> none  [the longest x1 14.1 us: on_device(): jax.nn.log_softmax(teacher_logits.astype(jnp.float32), axis=-1)]
    conv_general_dilated x9 -> x0, local copies, waits for them, and re-layouts: 14.6 us -> none  [lower_part(): lax.conv_general_dilated(gated, weight_depth[:, None, :], (1,), [(half_wi...]
  transfers between devices with their start and end apart: 2 -> 1, of which waited for: 1 -> 0; matrix products, arithmetic and copies ran while one was open for 13% -> 0% of each run, Pallas kernels for 0% -> 15%
where the time goes in v1:
time: 148 us
  Pallas kernels  141 us (95%)
  local copies, waits for them, and re-layouts  4.18 us (3%)
  starting transfers between devices  2.04 us (1%)
    pallas_call x1, Pallas kernels, reduce_all(): pl.pallas_call(reduce_kernel, name='reduce_all', out_shape=jax.ShapeDtype...  77.2 us
    pallas_call x1, Pallas kernels, compute(): bwd(lengths, own, got, logit, fn, z, rstd, act, fac, spec, s, a, normed,...  32.1 us
    pallas_call x1, Pallas kernels, compute(): fwd(lengths, features.reshape(TOK, D), g1, weight_in, weight_depth, weigh...  22.8 us
    pallas_call x1, Pallas kernels, finish(): pl.pallas_call(finish_kernel, name='finish', grid=(8,), out_shape=(sd((D,...  9.02 us
  transfers between devices with their start and end apart: 1, of which 0 were waited for; matrix products, arithmetic and copies ran while one was open for 0% of the time, Pallas kernels for 15%

profile of v1, /device:TPU:1, one launch (start us, length us, event | category | flops | bytes accessed | tf_op | source)
XLA Modules:
  0.0 148.0 jit_solution(2653317656799835518)
XLA Ops:
  0.6 2.1 %constant_dynamic-slice_fusion = (bf16[2,2,256,256]{3,2,1,0:T(8,128)(2,1)S(1)}, bf16[2,2,256,256]{3,2,1,0:T(8,128)(2,1)}) fusion(bf16[2,4,256,256]{3,2,1,0:T(8,128)(2,1)} %param.14, s32[]{:T(128)S(6)} %select_n.7, s32[]{:T(128)S(6)} %select_n.6), kind=kLoop, calls=%fused_computation.1 | loop fusion | bytes 2097160 | tf_op jit(solution)/shard_map/dynamic_slice | solution.py:533
  2.7 2.0 %collective-permute-start = (bf16[2,2,256,256]{3,2,1,0:T(8,128)(2,1)S(1)}, bf16[2,2,256,256]{3,2,1,0:T(8,128)(2,1)S(1)}, u32[]{:S(2)}, u32[]{:S(2)}) collective-permute-start(bf16[2,2,256,256]{3,2,1,0:T(8,128)(2,1)S(1)} %get-tuple-element.45), channel_id=1, source_target_pairs={{0,64},{64,0},{1,65},{65,1},{2,66},{66,2},{3,67},{67,3},{4,68},{68... | collective-permute-start | bytes 1572872 | tf_op jit(solution)/shard_map/ppermute | solution.py:535
  4.8 22.8 %forward.1 = (bf16[512,1024]{1,0:T(8,128)(2,1)}, bf16[512,1024]{1,0:T(8,128)(2,1)}, bf16[512,1024]{1,0:T(8,128)(2,1)}, bf16[2,288,1024]{2,1,0:T(8,128)(2,1)}, bf...) custom-call(s32[2]{0:T(128)} %len_ref.3, ...), custom_call_target="tpu_custom_call" | custom-call | flops 4000000000 | bytes 20971520 | tf_op jit(solution)/shard_map/forward/pallas_call | solution.py:273
  27.6 0.0 collective-permute-done.got_ref
  27.6 0.0 copy-start
  27.6 0.8 copy-done
  28.4 32.1 %backward.1 = (bf16[28,1024,128]{2,1,0:T(8,128)(2,1)}, f32[2,128]{1,0:T(2,128)}) custom-call(s32[2]{0:T(128)} %len_ref.3, bf16[2,2,256,256]{3,2,1,0:T(8,128)(2,1)} %get-tuple-element.46.own_ref, bf16[2,2,256,256]{3,2,1,0:T(8,128)(2,1)} %copy-done, f32[512,256]{1,0:T(8,128)} %get-tuple-element.26.logit_ref, bf16[512,1024]{1,0:T(8,128)(2,1)} %get-tuple-element.27.fn_ref, ...), custom_call_target="tpu_custom_call" | custom-call | tf_op jit(solution)/shard_map/backward/pallas_call | solution.py:290
  60.4 77.2 %reduce_all.1.in_ref.mid_ref.head_ref.small_ref = bf16[28,1024,128]{2,1,0:T(8,128)(2,1)} custom-call(bf16[28,1024,128]{2,1,0:T(8,128)(2,1)} %get-tuple-element.36.grad_ref), custom_call_target="tpu_custom_call" | custom-call | tf_op jit(solution)/shard_map/reduce_all/pallas_call | solution.py:455
  137.6 9.0 %finish.1 = (f32[1024,2048]{1,0:T(8,128)}, f32[1024,1024]{1,0:T(8,128)}, f32[1024,256]{1,0:T(8,128)}, f32[31,1024]{1,0:T(8,128)}, f32[1,1024]{1,0:T(1,128)}, /*index=5*/f32[1,1024]{1,0:T(1,128)}, f32[2,128]{1,0:T(2,128)}) custom-call(bf16[28,1024,128]{2,1,0:T(8,128)(2,1)} %reduce_all.1.in_ref.mid_ref.head_ref.small_ref, ...), custom_call_target="tpu_custom_call" | custom-call | tf_op jit(solution)/shard_map/finish/pallas_call | solution.py:502
  146.7 1.3 slice_reduce_fusion
Async XLA Ops:
  2.7 24.8 %collective-permute-start = (bf16[2,2,256,256]{3,2,1,0:T(8,128)(2,1)S(1)}, bf16[2,2,256,256]{3,2,1,0:T(8,128)(2,1)S(1)}, u32[]{:S(2)}, u32[]{:S(2)}) collective-permute-start(bf16[2,2,256,256]{3,2,1,0:T(8,128)(2,1)S(1)} %get-tuple-element.45), channel_id=1, source_target_pairs={{0,64},{64,0},{1,65},{65,1},{2,66},{66,2},{3,67},{67,3},{4,68},{68... | collective-permute-start | bytes 1572872 | tf_op jit(solution)/shard_map/ppermute | solution.py:535
  27.6 0.8 copy-start

commit v2 on v1

--- a/solution.py
+++ b/solution.py
@@ -294,8 +294,9 @@
 
 
 MESH = pl.DeviceIdType.MESH
-COUNTS = (3, 3, 2, 2, 2, 2)
-OFFSETS = (0, 3, 6, 8, 10, 12)
+STREAMS = 12
+COUNTS = (2, 1, 1, 1, 1, 1, 1, 2, 1, 1, 1, 1)
+OFFSETS = (0, 2, 3, 4, 5, 6, 7, 8, 10, 11, 12, 13)
 OWN = 14
 ROUNDS = 6
 
@@ -322,6 +323,7 @@
 
 
 def route(coords, core, s, k):
+    s = s % 6
     dim = (s // 2 + core + k // 2) % 3
     hit = [jnp.where(dim == d, 1, 0) for d in range(3)]
     c = sum(h * v for h, v in zip(hit, coords))
@@ -357,7 +359,7 @@
 
     pending = []
     pairs = []
-    for s in range(6):
+    for s in range(STREAMS):
         off, n = OFFSETS[s], COUNTS[s]
         c = copy(
             grad_ref.at[pl.ds(theirs + off, n)], pair_buf.at[pl.ds(off, n)], pair_s.at[s], pair_r.at[s], partner
@@ -365,9 +367,9 @@
         c.start()
         pairs.append(c)
 
-    starts = [jnp.int32(0)] * 6
-    history = [[] for _ in range(6)]
-    flying = [None] * 6
+    starts = [jnp.int32(0)] * STREAMS
+    history = [[] for _ in range(STREAMS)]
+    flying = [None] * STREAMS
 
     def launch(s, k):
         half = 512 >> k
@@ -399,7 +401,7 @@
 
         lax.fori_loop(0, size // step, run, 0)
 
-    for s in range(6):
+    for s in range(STREAMS):
         off, n = OFFSETS[s], COUNTS[s]
         pairs[s].wait_recv()
         add(work, off, 0, grad_ref, mine + off, 0, pair_buf, off, n, D)
@@ -407,7 +409,7 @@
 
     for k in range(ROUNDS):
         half = 512 >> k
-        for s in range(6):
+        for s in range(STREAMS):
             off, n = OFFSETS[s], COUNTS[s]
             flying[s].wait_recv()
             if k + 1 < ROUNDS:
@@ -417,22 +419,34 @@
                 add(out_ref, mine + off, starts[s], work, off, starts[s], bufs[k], off, n, half)
                 gather(s, k, copy, out_ref, mine, starts, history, ag_s, ag_r, flying, pending)
 
+    handed = []
+
+    def hand(s, part, start):
+        span = pl.ds(pl.multiple_of(start, 16), 512)
+        slots = pl.ds(mine + OFFSETS[s], COUNTS[s])
+        c = copy(
+            out_ref.at[slots, span], out_ref.at[slots, span], fin_s.at[part, s], fin_r.at[part, s], partner
+        )
+        c.start()
+        handed.append(c)
+
     for k in range(ROUNDS - 1, -1, -1):
         half = 512 >> k
-        for s in range(6):
+        for s in range(STREAMS):
             flying[s].wait_recv()
             _, keep = route(coords, core, s, k)
-            starts[s] = starts[s] - keep * half
+            before = starts[s]
+            starts[s] = before - keep * half
             if k > 0:
                 gather(s, k - 1, copy, out_ref, mine, starts, history, ag_s, ag_r, flying, pending)
+                if k == 1:
+                    hand(s, 0, starts[s])
             else:
-                slots = pl.ds(mine + OFFSETS[s], COUNTS[s])
-                c = copy(out_ref.at[slots], out_ref.at[slots], fin_s.at[s], fin_r.at[s], partner)
-                c.start()
-                pending.append(c)
-                flying[s] = c
-    for s in range(6):
-        flying[s].wait_recv()
+                hand(s, 1, 512 - before)
+    for c in handed:
+        c.wait_recv()
+        c.wait_send()
+    for s in range(STREAMS):
         pairs[s].wait_send()
     for c in pending:
         c.wait_send()
@@ -460,7 +474,7 @@
         out_specs=VM,
         scratch_shapes=[pltpu.VMEM((OWN, D, 128), BF16)] * 2
         + [pltpu.VMEM((OWN, 512 >> k, 128), BF16) for k in range(ROUNDS)]
-        + [dma((6,)), dma((6,))] + [dma((6, ROUNDS))] * 4 + [dma((6,)), dma((6,))],
+        + [dma((STREAMS,))] * 2 + [dma((STREAMS, ROUNDS))] * 4 + [dma((2, STREAMS))] * 2,
         compiler_params=pltpu.CompilerParams(
             collective_id=0, has_side_effects=True, vmem_limit_bytes=48 << 20
         ),

time: 148 us -> 143 us (0.966)
  Pallas kernels: 141 us -> 136 us
    pallas_call x1, Pallas kernels: 77.2 us -> 71.8 us  [reduce_all(): pl.pallas_call(reduce_kernel, name='reduce_all', out_shape=jax.ShapeDtype...]
  transfers between devices with their start and end apart: 1 -> 1, of which waited for: 0 -> 0; matrix products, arithmetic and copies ran while one was open for 0% -> 0% of each run, Pallas kernels for 15% -> 16%
where the time goes in v2:
time: 143 us
  Pallas kernels  136 us (95%)
  local copies, waits for them, and re-layouts  4.18 us (3%)
  starting transfers between devices  2.04 us (1%)
    pallas_call x1, Pallas kernels, reduce_all(): pl.pallas_call(reduce_kernel, name='reduce_all', out_shape=jax.ShapeDtype...  71.8 us
    pallas_call x1, Pallas kernels, compute(): bwd(lengths, own, got, logit, fn, z, rstd, act, fac, spec, s, a, normed,...  32.1 us
    pallas_call x1, Pallas kernels, compute(): fwd(lengths, features.reshape(TOK, D), g1, weight_in, weight_depth, weigh...  22.8 us
    pallas_call x1, Pallas kernels, finish(): pl.pallas_call(finish_kernel, name='finish', grid=(8,), out_shape=(sd((D,...  9.02 us
  transfers between devices with their start and end apart: 1, of which 0 were waited for; matrix products, arithmetic and copies ran while one was open for 0% of the time, Pallas kernels for 16%

profile of v2, /device:TPU:1, one launch (start us, length us, event | category | flops | bytes accessed | tf_op | source)
XLA Modules:
  0.0 142.5 jit_solution(8378775068785288143)
XLA Ops:
  0.6 2.1 %constant_dynamic-slice_fusion = (bf16[2,2,256,256]{3,2,1,0:T(8,128)(2,1)S(1)}, bf16[2,2,256,256]{3,2,1,0:T(8,128)(2,1)}) fusion(bf16[2,4,256,256]{3,2,1,0:T(8,128)(2,1)} %param.14, s32[]{:T(128)S(6)} %select_n.7, s32[]{:T(128)S(6)} %select_n.6), kind=kLoop, calls=%fused_computation.1 | loop fusion | bytes 2097160 | tf_op jit(solution)/shard_map/dynamic_slice | solution.py:547
  2.7 2.0 %collective-permute-start = (bf16[2,2,256,256]{3,2,1,0:T(8,128)(2,1)S(1)}, bf16[2,2,256,256]{3,2,1,0:T(8,128)(2,1)S(1)}, u32[]{:S(2)}, u32[]{:S(2)}) collective-permute-start(bf16[2,2,256,256]{3,2,1,0:T(8,128)(2,1)S(1)} %get-tuple-element.45), channel_id=1, source_target_pairs={{0,64},{64,0},{1,65},{65,1},{2,66},{66,2},{3,67},{67,3},{4,68},{68... | collective-permute-start | bytes 1572872 | tf_op jit(solution)/shard_map/ppermute | solution.py:549
  4.8 22.8 %forward.1 = (bf16[512,1024]{1,0:T(8,128)(2,1)}, bf16[512,1024]{1,0:T(8,128)(2,1)}, bf16[512,1024]{1,0:T(8,128)(2,1)}, bf16[2,288,1024]{2,1,0:T(8,128)(2,1)}, bf...) custom-call(s32[2]{0:T(128)} %len_ref.3, ...), custom_call_target="tpu_custom_call" | custom-call | flops 4000000000 | bytes 20971520 | tf_op jit(solution)/shard_map/forward/pallas_call | solution.py:273
  27.6 0.0 collective-permute-done.got_ref
  27.6 0.0 copy-start
  27.6 0.8 copy-done
  28.4 32.1 %backward.1 = (bf16[28,1024,128]{2,1,0:T(8,128)(2,1)}, f32[2,128]{1,0:T(2,128)}) custom-call(s32[2]{0:T(128)} %len_ref.3, bf16[2,2,256,256]{3,2,1,0:T(8,128)(2,1)} %get-tuple-element.46.own_ref, bf16[2,2,256,256]{3,2,1,0:T(8,128)(2,1)} %copy-done, f32[512,256]{1,0:T(8,128)} %get-tuple-element.26.logit_ref, bf16[512,1024]{1,0:T(8,128)(2,1)} %get-tuple-element.27.fn_ref, ...), custom_call_target="tpu_custom_call" | custom-call | tf_op jit(solution)/shard_map/backward/pallas_call | solution.py:290
  60.4 71.8 %reduce_all.1.in_ref.mid_ref.head_ref.small_ref = bf16[28,1024,128]{2,1,0:T(8,128)(2,1)} custom-call(bf16[28,1024,128]{2,1,0:T(8,128)(2,1)} %get-tuple-element.36.grad_ref), custom_call_target="tpu_custom_call" | custom-call | tf_op jit(solution)/shard_map/reduce_all/pallas_call | solution.py:469
  132.2 9.0 %finish.1 = (f32[1024,2048]{1,0:T(8,128)}, f32[1024,1024]{1,0:T(8,128)}, f32[1024,256]{1,0:T(8,128)}, f32[31,1024]{1,0:T(8,128)}, f32[1,1024]{1,0:T(1,128)}, /*index=5*/f32[1,1024]{1,0:T(1,128)}, f32[2,128]{1,0:T(2,128)}) custom-call(bf16[28,1024,128]{2,1,0:T(8,128)(2,1)} %reduce_all.1.in_ref.mid_ref.head_ref.small_ref, ...), custom_call_target="tpu_custom_call" | custom-call | tf_op jit(solution)/shard_map/finish/pallas_call | solution.py:516
  141.2 1.3 slice_reduce_fusion
Async XLA Ops:
  2.7 24.8 %collective-permute-start = (bf16[2,2,256,256]{3,2,1,0:T(8,128)(2,1)S(1)}, bf16[2,2,256,256]{3,2,1,0:T(8,128)(2,1)S(1)}, u32[]{:S(2)}, u32[]{:S(2)}) collective-permute-start(bf16[2,2,256,256]{3,2,1,0:T(8,128)(2,1)S(1)} %get-tuple-element.45), channel_id=1, source_target_pairs={{0,64},{64,0},{1,65},{65,1},{2,66},{66,2},{3,67},{67,3},{4,68},{68... | collective-permute-start | bytes 1572872 | tf_op jit(solution)/shard_map/ppermute | solution.py:549
  27.6 0.8 copy-start

commit v3 on v2

--- a/solution.py
+++ b/solution.py
@@ -14,6 +14,8 @@
 PERIOD, HALF, ROWS = 272, 144, 288
 TILE = 256
 SLABS = 28
+OWN = 14
+OUT_SLOT, HEAD_SLOT, SMALL_SLOT = 8, 12, 13
 F32, BF16 = jnp.float32, jnp.bfloat16
 VM = pl.BlockSpec(memory_space=pltpu.VMEM)
 SM = pl.BlockSpec(memory_space=pltpu.SMEM)
@@ -135,9 +137,21 @@
 def backward_kernel(
     len_ref, own_ref, got_ref, logit_ref, fn_ref, z_ref, rstd_ref, act_ref, fac_ref, spec_ref, s_ref, a_ref,
     normed_ref, win_ref, taps_ref, wout_ref, g2_ref, head_ref, tm_ref, c_ref, ct_ref, lag_ref,
-    grad_ref, loss_ref,
-    taps32, dl, dz, dr, dp, gain1, left,
+    grad_ref, loss_ref, pair_ref,
+    taps32, dl, dz, dr, dp, gain1, left, pair_s, pair_r,
 ):
+    coords, core = position()
+    partner = device(coords, 1 - core)
+    theirs = (1 - core) * OWN
+    barrier = pltpu.get_barrier_semaphore()
+    pl.semaphore_signal(barrier, inc=1, device_id=partner, device_id_type=MESH)
+
+    def handover(slot, n, sem):
+        return pltpu.make_async_remote_copy(
+            src_ref=grad_ref.at[pl.ds(theirs + slot, n)], dst_ref=pair_ref.at[pl.ds(slot, n)],
+            send_sem=pair_s.at[sem], recv_sem=pair_r.at[sem], device_id=partner, device_id_type=MESH,
+        )
+
     taps32[...] = jnp.zeros_like(taps32)
     taps32[0:TAPS, :] = taps_ref[...]
     gain1[...] = jnp.zeros_like(gain1)
@@ -172,14 +186,17 @@
         rows = cols
         dz[:, cols] = dot_bt(dl[...], head_ref[rows, :])
         dh = dot_at(fn_ref[:, cols], dl[...])
-        grad_ref[24, rows, :] = dh[:, :128].astype(BF16)
-        grad_ref[25, rows, :] = dh[:, 128:].astype(BF16)
+        grad_ref[HEAD_SLOT, rows, :] = dh[:, :128].astype(BF16)
+        grad_ref[OWN + HEAD_SLOT, rows, :] = dh[:, 128:].astype(BF16)
         left[1, rows, :] = jnp.broadcast_to(
             jnp.sum(dh * head_ref[rows, :].astype(F32), axis=-1, keepdims=True), (TILE, 128)
         )
         return carry
 
     lax.fori_loop(0, D // TILE, head_tile, 0)
+    pl.semaphore_wait(barrier, 1)
+    copies = [handover(HEAD_SLOT, 1, 4)]
+    copies[0].start()
 
     def norm_rows(rows, i):
         g = dz[rows, :] * g2_ref[...]
@@ -219,21 +236,34 @@
         left[0, cols, :] = dot_at(q.astype(BF16), lag_ref[...])
         dw = dot_at(act_ref[:, cols], dr[...])
         for j in range(8):
-            grad_ref[16 + j, cols, :] = dw[:, j * 128 : (j + 1) * 128].astype(BF16)
+            grad_ref[OUT_SLOT + j % 4 + OWN * (j // 4), cols, :] = dw[:, j * 128 : (j + 1) * 128].astype(BF16)
         return carry
 
     lax.fori_loop(0, D // TILE, conv_tile, 0)
-
-    def in_tile(n, carry):
+    copies.append(handover(OUT_SLOT, 4, 5))
+    copies[1].start()
+
+    def in_tile(group, i):
+        n = group * 4 + i
+        slot = group * OWN + 2 * i
         cols = pl.ds(pl.multiple_of(n * TILE, TILE), TILE)
         dw = dot_at(normed_ref[...], dp[:, cols])
-        grad_ref[2 * n] = dw[:, :128].astype(BF16)
-        grad_ref[2 * n + 1] = dw[:, 128:].astype(BF16)
+        grad_ref[slot] = dw[:, :128].astype(BF16)
+        grad_ref[slot + 1] = dw[:, 128:].astype(BF16)
         w = dw * win_ref[:, cols].astype(F32)
         gain1[...] += w[:, :128] + w[:, 128:]
+
+    def away(i, carry):
+        in_tile(1 - core, i)
+        handover(2 * i, 2, i).start()
         return carry
 
-    lax.fori_loop(0, 2 * D // TILE, in_tile, 0)
+    def home(i, carry):
+        in_tile(core, i)
+        return carry
+
+    lax.fori_loop(0, 4, away, 0)
+    lax.fori_loop(0, 4, home, 0)
 
     count = len_ref[0] + len_ref[1]
 
@@ -245,10 +275,17 @@
         out = jnp.where(lane == 32, g1, out)
         out = jnp.where(lane == 33, left[1, rows, :], out)
         out = jnp.where((lane >= 64) & (lane < 74), bit.astype(F32), out)
-        grad_ref[26, rows, :] = out.astype(BF16)
-        grad_ref[27, rows, :] = jnp.zeros((128, 128), BF16)
+        grad_ref[SMALL_SLOT, rows, :] = out.astype(BF16)
+        grad_ref[OWN + SMALL_SLOT, rows, :] = jnp.zeros((128, 128), BF16)
 
     rows_loop(D, 128, small_rows)
+    copies.append(handover(SMALL_SLOT, 1, 6))
+    copies[2].start()
+    for i in range(4):
+        copies.append(handover(2 * i, 2, i))
+    for c in copies:
+        c.wait_recv()
+        c.wait_send()
 
 
 def compute(features, own, got, lengths, gain_conv, weight_in, weight_depth, weight_out, gain_out, head):
@@ -277,15 +314,17 @@
     bwd = pl.pallas_call(
         backward_kernel,
         name="backward",
-        out_shape=(sd((SLABS, D, 128), BF16), sd((UTT, 128), F32)),
+        out_shape=(sd((SLABS, D, 128), BF16), sd((UTT, 128), F32), sd((OWN, D, 128), BF16)),
         in_specs=[SM] + [VM] * 21,
-        out_specs=[VM] * 2,
+        out_specs=[VM] * 3,
         scratch_shapes=[
             pltpu.VMEM((32, D), F32), pltpu.VMEM((TOK, V), BF16), pltpu.VMEM((TOK, D), F32),
             pltpu.VMEM((TOK, D), BF16), pltpu.VMEM((TOK, 2 * D), BF16), pltpu.VMEM((D, 128), F32),
-            pltpu.VMEM((2, D, 128), F32),
+            pltpu.VMEM((2, D, 128), F32), pltpu.SemaphoreType.DMA((7,)), pltpu.SemaphoreType.DMA((7,)),
         ],
-        compiler_params=cp,
+        compiler_params=pltpu.CompilerParams(
+            collective_id=1, has_side_effects=True, vmem_limit_bytes=60 << 20
+        ),
     )
     return bwd(
         lengths, own, got, logit, fn, z, rstd, act, fac, spec, s, a, normed, weight_in, weight_depth,
@@ -297,7 +336,6 @@
 STREAMS = 12
 COUNTS = (2, 1, 1, 1, 1, 1, 1, 2, 1, 1, 1, 1)
 OFFSETS = (0, 2, 3, 4, 5, 6, 7, 8, 10, 11, 12, 13)
-OWN = 14
 ROUNDS = 6
 
 
@@ -334,14 +372,13 @@
 
 
 def reduce_kernel(
-    grad_ref, out_ref, pair_buf, work, *rest
+    grad_ref, pair_buf, out_ref, work, *rest
 ):
     bufs = rest[:ROUNDS]
-    pair_s, pair_r, rs_s, rs_r, ag_s, ag_r, fin_s, fin_r = rest[ROUNDS:]
+    rs_s, rs_r, ag_s, ag_r, fin_s, fin_r = rest[ROUNDS:]
     coords, core = position()
     partner = device(coords, 1 - core)
     mine = core * OWN
-    theirs = (1 - core) * OWN
 
     barrier = pltpu.get_barrier_semaphore()
     greet = [partner]
@@ -350,7 +387,6 @@
             greet.append(device([other(v, wide) if i == d else v for i, v in enumerate(coords)], core))
     for dev in greet:
         pl.semaphore_signal(barrier, inc=1, device_id=dev, device_id_type=MESH)
-    pl.semaphore_wait(barrier, len(greet))
 
     def copy(src, dst, send, recv, dev):
         return pltpu.make_async_remote_copy(
@@ -358,14 +394,6 @@
         )
 
     pending = []
-    pairs = []
-    for s in range(STREAMS):
-        off, n = OFFSETS[s], COUNTS[s]
-        c = copy(
-            grad_ref.at[pl.ds(theirs + off, n)], pair_buf.at[pl.ds(off, n)], pair_s.at[s], pair_r.at[s], partner
-        )
-        c.start()
-        pairs.append(c)
 
     starts = [jnp.int32(0)] * STREAMS
     history = [[] for _ in range(STREAMS)]
@@ -403,8 +431,9 @@
 
     for s in range(STREAMS):
         off, n = OFFSETS[s], COUNTS[s]
-        pairs[s].wait_recv()
         add(work, off, 0, grad_ref, mine + off, 0, pair_buf, off, n, D)
+        if s == 0:
+            pl.semaphore_wait(barrier, len(greet))
         launch(s, 0)
 
     for k in range(ROUNDS):
@@ -446,8 +475,6 @@
     for c in handed:
         c.wait_recv()
         c.wait_send()
-    for s in range(STREAMS):
-        pairs[s].wait_send()
     for c in pending:
         c.wait_send()
 
@@ -464,25 +491,25 @@
     pending.append(c)
 
 
-def reduce_all(grads):
+def reduce_all(grads, pair):
     dma = pltpu.SemaphoreType.DMA
     return pl.pallas_call(
         reduce_kernel,
         name="reduce_all",
         out_shape=jax.ShapeDtypeStruct((SLABS, D, 128), BF16),
-        in_specs=[VM],
+        in_specs=[VM, VM],
         out_specs=VM,
-        scratch_shapes=[pltpu.VMEM((OWN, D, 128), BF16)] * 2
+        scratch_shapes=[pltpu.VMEM((OWN, D, 128), BF16)]
         + [pltpu.VMEM((OWN, 512 >> k, 128), BF16) for k in range(ROUNDS)]
-        + [dma((STREAMS,))] * 2 + [dma((STREAMS, ROUNDS))] * 4 + [dma((2, STREAMS))] * 2,
+        + [dma((STREAMS, ROUNDS))] * 4 + [dma((2, STREAMS))] * 2,
         compiler_params=pltpu.CompilerParams(
             collective_id=0, has_side_effects=True, vmem_limit_bytes=48 << 20
         ),
-    )(grads)
+    )(grads, pair)
 
 
 def finish_kernel(
-    in_ref, mid_ref, head_ref, small_ref, loss_ref, g1_ref, g2_ref,
+    in_ref, mid_ref, left_ref, right_ref, small_ref, loss_ref, g1_ref, g2_ref,
     win_ref, wout_ref, hw_ref, depth_ref, gain1_ref, gain2_ref, utt_ref, scale,
 ):
     @pl.when(pl.program_id(0) == 0)
@@ -503,7 +530,8 @@
     inv = scale[0:1, :]
     for j in range(2):
         win_ref[:, j * 128 : (j + 1) * 128] = in_ref[j].astype(F32) * inv
-        hw_ref[:, j * 128 : (j + 1) * 128] = head_ref[j].astype(F32) * inv
+        head = (left_ref, right_ref)[j]
+        hw_ref[:, j * 128 : (j + 1) * 128] = head[0].astype(F32) * inv
     wout_ref[...] = mid_ref[0].astype(F32) * inv
 
 
@@ -522,10 +550,11 @@
             sd((1, D), F32), sd((1, D), F32), sd((UTT, 128), F32),
         ),
         in_specs=[
-            pl.BlockSpec((2, D, 128), lambda i: (i, 0, 0)),
-            pl.BlockSpec((1, D, 128), lambda i: (16 + i, 0, 0)),
-            pl.BlockSpec((2, 128, 128), lambda i: (12, i, 0)),
-            pl.BlockSpec((1, D, 128), lambda i: (26, 0, 0)),
+            pl.BlockSpec((2, D, 128), lambda i: (i + 3 * (i // 4), 0, 0)),
+            pl.BlockSpec((1, D, 128), lambda i: (OUT_SLOT + i + 10 * (i // 4), 0, 0)),
+            pl.BlockSpec((1, 128, 128), lambda i: (HEAD_SLOT, i, 0)),
+            pl.BlockSpec((1, 128, 128), lambda i: (OWN + HEAD_SLOT, i, 0)),
+            pl.BlockSpec((1, D, 128), lambda i: (SMALL_SLOT, 0, 0)),
             whole(UTT, 128), whole(1, D), whole(1, D),
         ],
         out_specs=[
@@ -535,7 +564,7 @@
             whole(TAPS, D), whole(1, D), whole(1, D), whole(UTT, 128),
         ],
         scratch_shapes=[pltpu.VMEM((8, 128), F32)],
-    )(total, total, total, total, loss, gain_conv.reshape(1, D), gain_out.reshape(1, D))
+    )(total, total, total, total, total, loss, gain_conv.reshape(1, D), gain_out.reshape(1, D))
     win, wout, hw, depth, gain1, gain2, utt = outs
     return gain1.reshape(D), win, depth, wout, gain2.reshape(D), hw, utt[:, 0]
 
@@ -547,10 +576,10 @@
     give = lax.dynamic_slice_in_dim(teacher_logits, (1 - member) * UTT, UTT, 1)
     own = lax.dynamic_slice_in_dim(teacher_logits, member * UTT, UTT, 1)
     got = lax.ppermute(give, "member", ((0, 1), (1, 0)))
-    grads, loss = compute(
+    grads, loss, pair = compute(
         features, own, got, lengths, gain_conv, weight_in, weight_depth, weight_out, gain_out, head_weight
     )
-    return finish(reduce_all(grads), loss, gain_conv, gain_out)
+    return finish(reduce_all(grads, pair), loss, gain_conv, gain_out)
 
 
 def solution(mesh):

time: 143 us -> 146 us (1.021)
  local copies, waits for them, and re-layouts: 4.18 us -> 6.21 us
    pallas_call x1, Pallas kernels: 32.1 us -> 35.4 us  [compute(): bwd(lengths, own, got, logit, fn, z, rstd, act, fac, spec, s, a, normed,...]
    pallas_call x1, Pallas kernels: 71.8 us -> 69.2 us  [reduce_all(): pl.pallas_call(reduce_kernel, name='reduce_all', out_shape=jax.ShapeDtype...]
    unnamed x2 -> x4, local copies, waits for them, and re-layouts: 0.8 us -> 2.82 us
where the time goes in v3:
time: 146 us; the launch traced here: 145 us
  Pallas kernels  136 us (93%)
  local copies, waits for them, and re-layouts  6.21 us (4%)
  starting transfers between devices  2.04 us (1%)
    pallas_call x1, Pallas kernels, reduce_all(): pl.pallas_call(reduce_kernel, name='reduce_all', out_shape=jax.ShapeDtype...  69.2 us
    pallas_call x1, Pallas kernels, compute(): bwd(lengths, own, got, logit, fn, z, rstd, act, fac, spec, s, a, normed,...  35.4 us
    pallas_call x1, Pallas kernels, compute(): fwd(lengths, features.reshape(TOK, D), g1, weight_in, weight_depth, weigh...  22.8 us
    pallas_call x1, Pallas kernels, finish(): pl.pallas_call(finish_kernel, name='finish', grid=(8,), out_shape=(sd((D,...  9.12 us
  transfers between devices with their start and end apart: 1, of which 0 were waited for; matrix products, arithmetic and copies ran while one was open for 0% of the time, Pallas kernels for 16%

profile of v3, /device:TPU:1, one launch (start us, length us, event | category | flops | bytes accessed | tf_op | source)
XLA Modules:
  0.0 145.4 jit_solution(10706685089560338172)
XLA Ops:
  0.6 2.1 %constant_dynamic-slice_fusion = (bf16[2,2,256,256]{3,2,1,0:T(8,128)(2,1)S(1)}, bf16[2,2,256,256]{3,2,1,0:T(8,128)(2,1)}) fusion(bf16[2,4,256,256]{3,2,1,0:T(8,128)(2,1)} %param.14, s32[]{:T(128)S(6)} %select_n.7, s32[]{:T(128)S(6)} %select_n.6), kind=kLoop, calls=%fused_computation.1 | loop fusion | bytes 2097160 | tf_op jit(solution)/shard_map/dynamic_slice | solution.py:576
  2.7 2.0 %collective-permute-start = (bf16[2,2,256,256]{3,2,1,0:T(8,128)(2,1)S(1)}, bf16[2,2,256,256]{3,2,1,0:T(8,128)(2,1)S(1)}, u32[]{:S(2)}, u32[]{:S(2)}) collective-permute-start(bf16[2,2,256,256]{3,2,1,0:T(8,128)(2,1)S(1)} %get-tuple-element.47), channel_id=1, source_target_pairs={{0,64},{64,0},{1,65},{65,1},{2,66},{66,2},{3,67},{67,3},{4,68},{68... | collective-permute-start | bytes 1572872 | tf_op jit(solution)/shard_map/ppermute | solution.py:578
  4.8 22.8 %forward.1 = (bf16[512,1024]{1,0:T(8,128)(2,1)}, bf16[512,1024]{1,0:T(8,128)(2,1)}, bf16[512,1024]{1,0:T(8,128)(2,1)}, bf16[2,288,1024]{2,1,0:T(8,128)(2,1)}, bf...) custom-call(s32[2]{0:T(128)} %len_ref.3, ...), custom_call_target="tpu_custom_call" | custom-call | flops 4000000000 | bytes 20971520 | tf_op jit(solution)/shard_map/forward/pallas_call | solution.py:310
  27.6 0.0 collective-permute-done.got_ref
  27.6 0.0 copy-start.1
  27.6 0.8 copy-done.1
  28.4 35.4 %backward.1 = (bf16[28,1024,128]{2,1,0:T(8,128)(2,1)}, f32[2,128]{1,0:T(2,128)}, bf16[14,1024,128]{2,1,0:T(8,128)(2,1)}) custom-call(s32[2]{0:T(128)} %len_ref.3, bf16[2,2,256,256]{3,2,1,0:T(8,128)(2,1)} %get-tuple-element.48.own_ref, bf16[2,2,256,256]{3,2,1,0:T(8,128)(2,1)} %copy-done.1, f32[512,256]{1,0:T(8,128)} %get-tuple-element.27.logit_ref, ...), custom_call_target="tpu_custom_call" | custom-call | tf_op jit(solution)/shard_map/backward/pallas_call | solution.py:329
  63.8 0.0 copy-start
  63.8 2.0 %copy-done = bf16[14,1024,128]{2,1,0:T(8,128)(2,1)S(1)} copy-done((bf16[14,1024,128]{2,1,0:T(8,128)(2,1)S(1)}, bf16[14,1024,128]{2,1,0:T(8,128)(2,1)}, u32[]{:S(2)}) %copy-start) | copy-done | bytes 3670040
  65.8 69.2 %reduce_all.1.in_ref.mid_ref.left_ref.right_ref.small_ref = bf16[28,1024,128]{2,1,0:T(8,128)(2,1)} custom-call(bf16[28,1024,128]{2,1,0:T(8,128)(2,1)} %get-tuple-element.37.grad_ref, bf16[14,1024,128]{2,1,0:T(8,128)(2,1)S(1)} %copy-done), custom_call_target="tpu_custom_call" | custom-call | tf_op jit(solution)/shard_map/reduce_all/pallas_call | solution.py:496
  135.0 9.1 %finish.1 = (f32[1024,2048]{1,0:T(8,128)}, f32[1024,1024]{1,0:T(8,128)}, f32[1024,256]{1,0:T(8,128)}, f32[31,1024]{1,0:T(8,128)}, f32[1,1024]{1,0:T(1,128)}, /*index=5*/f32[1,1024]{1,0:T(1,128)}, f32[2,128]{1,0:T(2,128)}) custom-call(bf16[28,1024,128]{2,1,0:T(8,128)(2,1)} %reduce_all.1.in_ref.mid_ref.left_ref.right_ref.small_ref, ...), custom_call_target="tpu_custom_call" | custom-call | tf_op jit(solution)/shard_map/finish/pallas_call | solution.py:544
  144.1 1.3 slice_reduce_fusion
Async XLA Ops:
  2.7 24.9 %collective-permute-start = (bf16[2,2,256,256]{3,2,1,0:T(8,128)(2,1)S(1)}, bf16[2,2,256,256]{3,2,1,0:T(8,128)(2,1)S(1)}, u32[]{:S(2)}, u32[]{:S(2)}) collective-permute-start(bf16[2,2,256,256]{3,2,1,0:T(8,128)(2,1)S(1)} %get-tuple-element.47), channel_id=1, source_target_pairs={{0,64},{64,0},{1,65},{65,1},{2,66},{66,2},{3,67},{67,3},{4,68},{68... | collective-permute-start | bytes 1572872 | tf_op jit(solution)/shard_map/ppermute | solution.py:578
  27.6 0.8 copy-start.1
  63.8 2.0 %copy-start = (bf16[14,1024,128]{2,1,0:T(8,128)(2,1)S(1)}, bf16[14,1024,128]{2,1,0:T(8,128)(2,1)}, u32[]{:S(2)}) copy-start(bf16[14,1024,128]{2,1,0:T(8,128)(2,1)} %get-tuple-element.38.pair_buf) | copy-start | bytes 11010052

commit v4 on v2

--- a/solution.py
+++ b/solution.py
@@ -141,6 +141,7 @@
     taps32[...] = jnp.zeros_like(taps32)
     taps32[0:TAPS, :] = taps_ref[...]
     gain1[...] = jnp.zeros_like(gain1)
+    first = lax.axis_index("member") * UTT
 
     for u in range(UTT):
         length = len_ref[u]
@@ -151,7 +152,7 @@
             summed = jnp.zeros((32, V), F32)
             for ref in (own_ref, got_ref):
                 for k in range(2):
-                    t = ref[k, u, rows, :].astype(F32)
+                    t = ref[k, first + u, rows, :].astype(F32)
                     m, _, z = softmax_parts(t)
                     summed = summed + (t - m - jnp.log(z))
             _, e, z = softmax_parts(summed * 0.25)
@@ -494,7 +495,8 @@
         count = jnp.sum(jnp.where(used, first * place, 0.0), axis=-1, keepdims=True)
         inv = UTTS / count
         scale[...] = jnp.broadcast_to(inv, (8, 128))
-        utt_ref[...] = loss_ref[...] * inv
+        for u in range(UTT):
+            utt_ref[u] = jnp.max(loss_ref[u : u + 1, :] * inv)
         small = small_ref[0].astype(F32).T * inv
         depth_ref[...] = small[0:TAPS, :]
         gain1_ref[...] = small[32:33, :] / g1_ref[...]
@@ -519,7 +521,7 @@
         grid=(8,),
         out_shape=(
             sd((D, 2 * D), F32), sd((D, D), F32), sd((D, V), F32), sd((TAPS, D), F32),
-            sd((1, D), F32), sd((1, D), F32), sd((UTT, 128), F32),
+            sd((1, D), F32), sd((1, D), F32), sd((UTT,), F32),
         ),
         in_specs=[
             pl.BlockSpec((2, D, 128), lambda i: (i, 0, 0)),
@@ -532,23 +534,21 @@
             pl.BlockSpec((D, 256), lambda i: (0, i)),
             pl.BlockSpec((D, 128), lambda i: (0, i)),
             pl.BlockSpec((128, V), lambda i: (i, 0)),
-            whole(TAPS, D), whole(1, D), whole(1, D), whole(UTT, 128),
+            whole(TAPS, D), whole(1, D), whole(1, D), SM,
         ],
         scratch_shapes=[pltpu.VMEM((8, 128), F32)],
     )(total, total, total, total, loss, gain_conv.reshape(1, D), gain_out.reshape(1, D))
     win, wout, hw, depth, gain1, gain2, utt = outs
-    return gain1.reshape(D), win, depth, wout, gain2.reshape(D), hw, utt[:, 0]
+    return gain1.reshape(D), win, depth, wout, gain2.reshape(D), hw, utt
 
 
 def on_device(
     features, teacher_logits, lengths, gain_conv, weight_in, weight_depth, weight_out, gain_out, head_weight
 ):
-    member = lax.axis_index("member")
-    give = lax.dynamic_slice_in_dim(teacher_logits, (1 - member) * UTT, UTT, 1)
-    own = lax.dynamic_slice_in_dim(teacher_logits, member * UTT, UTT, 1)
-    got = lax.ppermute(give, "member", ((0, 1), (1, 0)))
+    got = lax.ppermute(teacher_logits, "member", ((0, 1), (1, 0)))
     grads, loss = compute(
-        features, own, got, lengths, gain_conv, weight_in, weight_depth, weight_out, gain_out, head_weight
+        features, teacher_logits, got, lengths, gain_conv, weight_in, weight_depth, weight_out, gain_out,
+        head_weight,
     )
     return finish(reduce_all(grads), loss, gain_conv, gain_out)
 

time: 143 us -> 141 us (0.986)
  local copies, waits for them, and re-layouts: 4.18 us -> 0.96 us
    dynamic_slice x1 -> x0, local copies, waits for them, and re-layouts: 2.07 us -> none  [on_device(): give = lax.dynamic_slice_in_dim(teacher_logits, (1 - member) * UTT, UTT, 1)]
where the time goes in v4:
time: 141 us
  Pallas kernels  137 us (97%)
  starting transfers between devices  2.12 us (2%)
    pallas_call x1, Pallas kernels, reduce_all(): pl.pallas_call(reduce_kernel, name='reduce_all', out_shape=jax.ShapeDtype...  73.1 us
    pallas_call x1, Pallas kernels, compute(): bwd(lengths, own, got, logit, fn, z, rstd, act, fac, spec, s, a, normed,...  32.4 us
    pallas_call x1, Pallas kernels, compute(): fwd(lengths, features.reshape(TOK, D), g1, weight_in, weight_depth, weigh...  22.8 us
    pallas_call x1, Pallas kernels, finish(): pl.pallas_call(finish_kernel, name='finish', grid=(8,), out_shape=(sd((D,...  9.08 us
  transfers between devices with their start and end apart: 1, of which 0 were waited for; matrix products, arithmetic and copies ran while one was open for 0% of the time, Pallas kernels for 16%

profile of v4, /device:TPU:1, one launch (start us, length us, event | category | flops | bytes accessed | tf_op | source)
XLA Modules:
  0.0 141.1 jit_solution(3557897315693588074)
XLA Ops:
  0.6 2.1 %collective-permute-start = (bf16[2,4,256,256]{3,2,1,0:T(8,128)(2,1)}, bf16[2,4,256,256]{3,2,1,0:T(8,128)(2,1)S(1)}, u32[]{:S(2)}, u32[]{:S(2)}) collective-permute-start(bf16[2,4,256,256]{3,2,1,0:T(8,128)(2,1)} %own_ref.1), channel_id=1, source_target_pairs={{0,64},{64,0},{1,65},{65,1},{2,66},{66,2},{3,67},{67,3},{4,68},{68... | collective-permute-start | bytes 3145736 | tf_op jit(solution)/shard_map/ppermute | solution.py:548
  2.8 22.8 %forward.1 = (bf16[512,1024]{1,0:T(8,128)(2,1)}, bf16[512,1024]{1,0:T(8,128)(2,1)}, bf16[512,1024]{1,0:T(8,128)(2,1)}, bf16[2,288,1024]{2,1,0:T(8,128)(2,1)}, bf...) custom-call(s32[2]{0:T(128)} %len_ref.3, ...), custom_call_target="tpu_custom_call" | custom-call | flops 4000000000 | bytes 20971520 | tf_op jit(solution)/shard_map/forward/pallas_call | solution.py:274
  25.6 0.0 collective-permute-done.got_ref
  25.6 0.0 copy-start
  25.6 1.0 copy-done
  26.5 32.4 %backward.1 = (bf16[28,1024,128]{2,1,0:T(8,128)(2,1)}, f32[2,128]{1,0:T(2,128)}) custom-call(s32[2]{0:T(128)} %len_ref.3, bf16[2,4,256,256]{3,2,1,0:T(8,128)(2,1)} %own_ref.1, bf16[2,4,256,256]{3,2,1,0:T(8,128)(2,1)} %copy-done, f32[512,256]{1,0:T(8,128)} %get-tuple-element.26.logit_ref, bf16[512,1024]{1,0:T(8,128)(2,1)} %get-tuple-element.27.fn_ref, ...), custom_call_target="tpu_custom_call" | custom-call | tf_op jit(solution)/shard_map/backward/pallas_call | solution.py:291
  58.9 73.1 %reduce_all.1.in_ref.mid_ref.head_ref.small_ref = bf16[28,1024,128]{2,1,0:T(8,128)(2,1)} custom-call(bf16[28,1024,128]{2,1,0:T(8,128)(2,1)} %get-tuple-element.36.grad_ref), custom_call_target="tpu_custom_call" | custom-call | tf_op jit(solution)/shard_map/reduce_all/pallas_call | solution.py:470
  132.0 9.1 %finish.1 = (f32[1024,2048]{1,0:T(8,128)}, f32[1024,1024]{1,0:T(8,128)}, f32[1024,256]{1,0:T(8,128)}, f32[31,1024]{1,0:T(8,128)}, f32[1,1024]{1,0:T(1,128)}, /*index=5*/f32[1,1024]{1,0:T(1,128)}, f32[2]{0:T(128)}) custom-call(bf16[28,1024,128]{2,1,0:T(8,128)(2,1)} %reduce_all.1.in_ref.mid_ref.head_ref.small_ref, ...), custom_call_target="tpu_custom_call" | custom-call | tf_op jit(solution)/shard_map/finish/pallas_call | solution.py:518
Async XLA Ops:
  0.6 24.9 %collective-permute-start = (bf16[2,4,256,256]{3,2,1,0:T(8,128)(2,1)}, bf16[2,4,256,256]{3,2,1,0:T(8,128)(2,1)S(1)}, u32[]{:S(2)}, u32[]{:S(2)}) collective-permute-start(bf16[2,4,256,256]{3,2,1,0:T(8,128)(2,1)} %own_ref.1), channel_id=1, source_target_pairs={{0,64},{64,0},{1,65},{65,1},{2,66},{66,2},{3,67},{67,3},{4,68},{68... | collective-permute-start | bytes 3145736 | tf_op jit(solution)/shard_map/ppermute | solution.py:548
  25.6 1.0 copy-start

commit v5 on v4

--- a/solution.py
+++ b/solution.py
@@ -503,10 +503,9 @@
         gain2_ref[...] = small[33:34, :] / g2_ref[...]
 
     inv = scale[0:1, :]
-    for j in range(2):
-        win_ref[:, j * 128 : (j + 1) * 128] = in_ref[j].astype(F32) * inv
-        hw_ref[:, j * 128 : (j + 1) * 128] = head_ref[j].astype(F32) * inv
-    wout_ref[...] = mid_ref[0].astype(F32) * inv
+    for src, dst, n in ((in_ref, win_ref, 16), (mid_ref, wout_ref, 8), (head_ref, hw_ref, 2)):
+        for j in range(n):
+            dst[:, j * 128 : (j + 1) * 128] = src[j].astype(F32) * inv
 
 
 UTTS = 256.0
@@ -524,15 +523,15 @@
             sd((1, D), F32), sd((1, D), F32), sd((UTT,), F32),
         ),
         in_specs=[
-            pl.BlockSpec((2, D, 128), lambda i: (i, 0, 0)),
-            pl.BlockSpec((1, D, 128), lambda i: (16 + i, 0, 0)),
+            pl.BlockSpec((16, 128, 128), lambda i: (0, i, 0)),
+            pl.BlockSpec((8, 128, 128), lambda i: (2, i, 0)),
             pl.BlockSpec((2, 128, 128), lambda i: (12, i, 0)),
             pl.BlockSpec((1, D, 128), lambda i: (26, 0, 0)),
             whole(UTT, 128), whole(1, D), whole(1, D),
         ],
         out_specs=[
-            pl.BlockSpec((D, 256), lambda i: (0, i)),
-            pl.BlockSpec((D, 128), lambda i: (0, i)),
+            pl.BlockSpec((128, 2 * D), lambda i: (i, 0)),
+            pl.BlockSpec((128, D), lambda i: (i, 0)),
             pl.BlockSpec((128, V), lambda i: (i, 0)),
             whole(TAPS, D), whole(1, D), whole(1, D), SM,
         ],

time: 141 us -> 142 us (level)
  no operation moved by 1% of the time
where the time goes in v5:
time: 142 us; the launch traced here: 141 us
  Pallas kernels  138 us (97%)
  starting transfers between devices  2.12 us (1%)
    pallas_call x1, Pallas kernels, reduce_all(): pl.pallas_call(reduce_kernel, name='reduce_all', out_shape=jax.ShapeDtype...  73.1 us
    pallas_call x1, Pallas kernels, compute(): bwd(lengths, own, got, logit, fn, z, rstd, act, fac, spec, s, a, normed,...  32.4 us
    pallas_call x1, Pallas kernels, compute(): fwd(lengths, features.reshape(TOK, D), g1, weight_in, weight_depth, weigh...  22.8 us
    pallas_call x1, Pallas kernels, finish(): pl.pallas_call(finish_kernel, name='finish', grid=(8,), out_shape=(sd((D,...  9.42 us
  transfers between devices with their start and end apart: 1, of which 0 were waited for; matrix products, arithmetic and copies ran while one was open for 0% of the time, Pallas kernels for 16%

profile of v5, /device:TPU:1, one launch (start us, length us, event | category | flops | bytes accessed | tf_op | source)
XLA Modules:
  0.0 141.4 jit_solution(13293062547246048638)
XLA Ops:
  0.6 2.1 %collective-permute-start = (bf16[2,4,256,256]{3,2,1,0:T(8,128)(2,1)}, bf16[2,4,256,256]{3,2,1,0:T(8,128)(2,1)S(1)}, u32[]{:S(2)}, u32[]{:S(2)}) collective-permute-start(bf16[2,4,256,256]{3,2,1,0:T(8,128)(2,1)} %own_ref.1), channel_id=1, source_target_pairs={{0,64},{64,0},{1,65},{65,1},{2,66},{66,2},{3,67},{67,3},{4,68},{68... | collective-permute-start | bytes 3145736 | tf_op jit(solution)/shard_map/ppermute | solution.py:547
  2.8 22.8 %forward.1 = (bf16[512,1024]{1,0:T(8,128)(2,1)}, bf16[512,1024]{1,0:T(8,128)(2,1)}, bf16[512,1024]{1,0:T(8,128)(2,1)}, bf16[2,288,1024]{2,1,0:T(8,128)(2,1)}, bf...) custom-call(s32[2]{0:T(128)} %len_ref.3, ...), custom_call_target="tpu_custom_call" | custom-call | flops 4000000000 | bytes 20971520 | tf_op jit(solution)/shard_map/forward/pallas_call | solution.py:274
  25.6 0.0 collective-permute-done.got_ref
  25.6 0.0 copy-start
  25.6 1.0 copy-done
  26.5 32.4 %backward.1 = (bf16[28,1024,128]{2,1,0:T(8,128)(2,1)}, f32[2,128]{1,0:T(2,128)}) custom-call(s32[2]{0:T(128)} %len_ref.3, bf16[2,4,256,256]{3,2,1,0:T(8,128)(2,1)} %own_ref.1, bf16[2,4,256,256]{3,2,1,0:T(8,128)(2,1)} %copy-done, f32[512,256]{1,0:T(8,128)} %get-tuple-element.26.logit_ref, bf16[512,1024]{1,0:T(8,128)(2,1)} %get-tuple-element.27.fn_ref, ...), custom_call_target="tpu_custom_call" | custom-call | tf_op jit(solution)/shard_map/backward/pallas_call | solution.py:291
  58.9 73.1 %reduce_all.1.in_ref.mid_ref.head_ref.small_ref = bf16[28,1024,128]{2,1,0:T(8,128)(2,1)} custom-call(bf16[28,1024,128]{2,1,0:T(8,128)(2,1)} %get-tuple-element.36.grad_ref), custom_call_target="tpu_custom_call" | custom-call | tf_op jit(solution)/shard_map/reduce_all/pallas_call | solution.py:470
  132.0 9.4 %finish.1 = (f32[1024,2048]{1,0:T(8,128)}, f32[1024,1024]{1,0:T(8,128)}, f32[1024,256]{1,0:T(8,128)}, f32[31,1024]{1,0:T(8,128)}, f32[1,1024]{1,0:T(1,128)}, /*index=5*/f32[1,1024]{1,0:T(1,128)}, f32[2]{0:T(128)}) custom-call(bf16[28,1024,128]{2,1,0:T(8,128)(2,1)} %reduce_all.1.in_ref.mid_ref.head_ref.small_ref, ...), custom_call_target="tpu_custom_call" | custom-call | tf_op jit(solution)/shard_map/finish/pallas_call | solution.py:517
Async XLA Ops:
  0.6 24.9 %collective-permute-start = (bf16[2,4,256,256]{3,2,1,0:T(8,128)(2,1)}, bf16[2,4,256,256]{3,2,1,0:T(8,128)(2,1)S(1)}, u32[]{:S(2)}, u32[]{:S(2)}) collective-permute-start(bf16[2,4,256,256]{3,2,1,0:T(8,128)(2,1)} %own_ref.1), channel_id=1, source_target_pairs={{0,64},{64,0},{1,65},{65,1},{2,66},{66,2},{3,67},{67,3},{4,68},{68... | collective-permute-start | bytes 3145736 | tf_op jit(solution)/shard_map/ppermute | solution.py:547
  25.6 1.0 copy-start
